TPU v7x, 256 devices: a whole 4x4x8 slice. The times are simulated.
256 devices in a mesh: expert: 64 (over y, z, core), ctx: 4 (over x).
Axes of the slice: x: 4, y: 4, z: 8, core: 2. Of those that a mesh axis runs over, the one named last changes fastest.
Arguments:
- resid: bfloat16 [32768, 2048], P(('expert', 'ctx')), may hold values from -30 to 30
- queries: bfloat16 [32768, 2048], P(('expert', 'ctx')), may hold values from -8 to 8
- keys: bfloat16 [32768, 2048], P(('expert', 'ctx')), may hold values from -8 to 8
- values: bfloat16 [32768, 2048], P(('expert', 'ctx')), may hold values from -6 to 6
- mod_scale: float32 [64, 2048], P('expert'), may hold values from -0.5 to 0.5
- mod_shift: float32 [64, 2048], P('expert'), may hold values from -3 to 3
- mod_gate: float32 [64, 2048], P('expert'), may hold values from 0.5 to 1.5
- router: bfloat16 [2048, 64], replicated, may hold values from -0.125 to 0.125
- w_in: bfloat16 [64, 2048, 1024], P('expert', None, 'ctx'), may hold values from -0.125 to 0.125
- w_out: bfloat16 [64, 1024, 2048], P('expert', 'ctx'), may hold values from -0.1875 to 0.1875
- expert_ids: int32 [32768, 2], P(('expert', 'ctx')), may hold values from 0 to 63, all different within a row; in each aligned block of 128 rows (0 to 127, 128 to 255, ...) at most 5 rows name the same one
- grad_out: bfloat16 [32768, 2048], P(('expert', 'ctx')), may hold values from -1.5 to 1.5
Outputs:
- mixed_out: bfloat16 [32768, 2048], P(('expert', 'ctx'))
- resid_grad: bfloat16 [32768, 2048], P(('expert', 'ctx'))
- grad_queries: bfloat16 [32768, 2048], P(('expert', 'ctx'))
- grad_keys: bfloat16 [32768, 2048], P(('expert', 'ctx'))
- grad_values: bfloat16 [32768, 2048], P(('expert', 'ctx'))
- grad_w_in: bfloat16 [64, 2048, 1024], P('expert', None, 'ctx')
- grad_w_out: bfloat16 [64, 1024, 2048], P('expert', 'ctx')
- grad_router: float32 [2048, 64], replicated
Inputs may be any that keep to these rules, and one draw needn't show every extreme that they name: `expert_ids`: each token names two different experts. Within one aligned block of 128 tokens no expert is named by more than 5 tokens, and some block reaches 5.
All inputs are finite; a program needn't handle non-finite values.
Results may differ from a plain program's by a relative error of at most 0.013.
The roundings to bfloat16 on the way count: a program that leaves them out, or rounds other values in their place, can miss the bound.
Values may be sent and summed in bfloat16 or wider, within the bound.
No kernel may reach another device: no remote copies, remote signals or barrier semaphores. Data moves between devices by JAX's collectives and lax.ppermute only.
A program may use at most 128 MiB of HBM per device.

v0:
```python
import math

import jax
import jax.numpy as jnp
from jax import lax
from jax.experimental import pallas as pl
from jax.experimental.pallas import tpu as pltpu
from jax.sharding import PartitionSpec as P

D = 2048
HEADS = 16
HDIM = 128
EXPERTS = 64
TOK = 128
CTX = 4
CAP = 5
SLOTS = EXPERTS * CAP
CHUNKS = D // 128
WIDE = 512
FF_BLOCK = 256
PLAIN = CAP * CHUNKS
TAGGED = PLAIN + 16
NORM_EPSILON = 1e-06
SCORE_SCALE = 1.0 / math.sqrt(HDIM)
GELU_C = math.sqrt(2.0 / math.pi)
BF = jnp.bfloat16
F32 = jnp.float32


def params(mib=44):
    return pltpu.CompilerParams(vmem_limit_bytes=mib << 20)


def dot(a, b):
    return jnp.dot(a, b, preferred_element_type=F32)


def dot_rows(a, b):
    return lax.dot_general(a, b, (((0,), (0,)), ((), ())), preferred_element_type=F32)


def dot_cols(a, b):
    return lax.dot_general(a, b, (((1,), (1,)), ((), ())), preferred_element_type=F32)


def shape(dims, kind):
    return jax.ShapeDtypeStruct(dims, kind)


def hbm(dims, kind):
    return pltpu.HBM(dims, kind)


def cost(micros):
    return pl.CostEstimate(flops=0, transcendentals=0, bytes_accessed=int(micros * 3e6))


SCALAR = pl.BlockSpec(memory_space=pltpu.SMEM)
IN_HBM = pl.BlockSpec(memory_space=pltpu.HBM)
FULL = pl.BlockSpec(memory_space=pltpu.VMEM)


def staged(body, scalars, args, out_shape, name, micros, scratch=(), unread=(), mib=44, carried=None):
    outs = list(out_shape) if isinstance(out_shape, (list, tuple)) else [out_shape]
    extra = {}
    if carried is not None:
        unread = [*unread, carried]
        outs = outs + [hbm(carried.shape, carried.dtype)]
        out_shape = outs
        extra = {
            "out_specs": [FULL] * (len(outs) - 1) + [IN_HBM],
            "input_output_aliases": {len(scalars) + len(args) + len(unread) - 1: len(outs) - 1},
        }
    front, read = len(scalars) + len(args), len(scalars) + len(args) + len(unread)

    def kernel(*refs):
        results = refs[read : read + len(outs)]
        own = refs[read + len(outs) : read + len(outs) + len(scratch)]
        buffers = refs[read + len(outs) + len(scratch) : -1]
        copies = [
            pltpu.make_async_copy(source, buffer, refs[-1].at[i])
            for i, (source, buffer) in enumerate(zip(refs[len(scalars) : front], buffers))
        ]
        for copy in copies:
            copy.start()
        for copy in copies:
            copy.wait()
        body(*refs[: len(scalars)], *buffers, *results, *own)

    return pl.pallas_call(
        kernel,
        in_specs=[SCALAR] * len(scalars) + [IN_HBM] * (len(args) + len(unread)),
        out_shape=out_shape,
        scratch_shapes=list(scratch)
        + [pltpu.VMEM(x.shape, x.dtype) for x in args]
        + [pltpu.SemaphoreType.DMA((len(args),))],
        compiler_params=params(mib),
        cost_estimate=cost(micros),
        name=name,
        **extra,
    )(*scalars, *args, *unread)


def ref_to_blocks(rows, stage):
    @pl.loop(0, CAP)
    def _(s):
        for c in range(CHUNKS):
            stage[pl.ds(s * CHUNKS + c, EXPERTS, stride=PLAIN), :] = rows[
                pl.ds(pl.multiple_of(s * EXPERTS, EXPERTS), EXPERTS), c * 128 : (c + 1) * 128
            ]


def store_blocks(stage, blocks):
    @pl.loop(0, EXPERTS // 8)
    def _(i):
        rows = stage[pl.ds(pl.multiple_of(i * 8 * PLAIN, 8 * PLAIN), 8 * PLAIN), :]
        blocks[pl.ds(pl.multiple_of(i * 8, 8), 8)] = rows.reshape(8, PLAIN, 128).astype(BF)


def from_blocks(blocks, stage, rows, block):
    @pl.loop(0, EXPERTS // 8)
    def _(i):
        stage[pl.ds(pl.multiple_of(i * 8 * block, 8 * block), 8 * block), :] = (
            blocks[pl.ds(pl.multiple_of(i * 8, 8), 8)].astype(F32).reshape(8 * block, 128)
        )

    @pl.loop(0, CAP)
    def _(s):
        for c in range(CHUNKS):
            rows[pl.ds(pl.multiple_of(s * EXPERTS, EXPERTS), EXPERTS), c * 128 : (c + 1) * 128] = stage[
                pl.ds(s * CHUNKS + c, EXPERTS, stride=block), :
            ].astype(BF)


def one_hot(column, width):
    return (column == lax.broadcasted_iota(jnp.int32, (column.shape[0], width), 1)).astype(F32)


def group_cols(place, s):
    return pl.ds(pl.multiple_of(lax.rem(place[0] + s, CTX) * WIDE, WIDE), WIDE)


def pack_body(place, q, k, v, *outs):
    for s, out in enumerate(outs):
        cols = group_cols(place, s)
        out[0:TOK] = q[:, cols]
        out[TOK : 2 * TOK] = k[:, cols]
        out[2 * TOK :] = v[:, cols]


def pack(group, q, k, v):
    return staged(pack_body, [group], [q, k, v], [hbm((3 * TOK, WIDE), BF)] * CTX, "pack_heads", 3)


def unpack_body(place, *refs):
    dq, dk, dv = refs[CTX:]
    for s in range(CTX):
        x, cols = refs[s], group_cols(place, s)
        dq[:, cols] = x[0:TOK]
        dk[:, cols] = x[TOK : 2 * TOK]
        dv[:, cols] = x[2 * TOK :]


def unpack(group, parts):
    return staged(unpack_body, [group], parts, [hbm((TOK, D), BF)] * 3, "unpack_heads", 60)


def tagged_store(out, stage, tag_rows):
    store_blocks(stage, out.at[:, 0:PLAIN, :])
    row = lax.broadcasted_iota(jnp.int32, (EXPERTS, 16, 128), 1)
    tags = jnp.zeros((EXPERTS, 16, 128), F32)
    for i, tag in enumerate(tag_rows):
        tags = jnp.where(row == i, tag[:, None, :], tags)
    out[:, PLAIN:, :] = tags.astype(BF)


def slots_to_lanes(columns):
    lane = lax.broadcasted_iota(jnp.int32, (EXPERTS, 128), 1)
    table = jnp.zeros((EXPERTS, 128), F32)
    for s in range(CAP):
        table = jnp.where(lane == s, columns[s * EXPERTS : (s + 1) * EXPERTS], table)
    return table


def grads_body(grad_out, mod_gate, ids, place_out, send, stage, picked):
    first, second = ids[:, 0:1], ids[:, 1:2]
    first_hot, second_hot = one_hot(first, EXPERTS), one_hot(second, EXPERTS)
    both = first_hot + second_hot
    rows = lax.broadcasted_iota(jnp.int32, (TOK, TOK), 0)
    cols = lax.broadcasted_iota(jnp.int32, (TOK, TOK), 1)
    earlier = dot((cols < rows).astype(BF), both.astype(BF))
    pos_one = jnp.sum(earlier * first_hot, axis=1, keepdims=True).astype(jnp.int32)
    pos_two = jnp.sum(earlier * second_hot, axis=1, keepdims=True).astype(jnp.int32)
    place_one = pos_one * EXPERTS + first
    place_two = pos_two * EXPERTS + second
    lane = lax.broadcasted_iota(jnp.int32, (TOK, 2), 1)
    place_out[...] = jnp.where(lane == 0, place_one, place_two)
    pick_one = one_hot(place_one, SLOTS).astype(BF)
    pick_two = one_hot(place_two, SLOTS).astype(BF)
    branch_grad = (mod_gate[...] * grad_out[...].astype(F32)).astype(BF)
    picked[...] = dot_rows(pick_one + pick_two, branch_grad)
    ref_to_blocks(picked, stage)
    other_one = jnp.broadcast_to(second.astype(F32), (TOK, 128)).astype(BF)
    other_two = jnp.broadcast_to(first.astype(F32), (TOK, 128)).astype(BF)
    partner = dot_rows(pick_one, other_one) + dot_rows(pick_two, other_two)
    tagged_store(send, stage, [slots_to_lanes(partner)])


def send_grads(grad_out, mod_gate, ids, after):
    return staged(
        grads_body,
        [],
        [grad_out, mod_gate, ids],
        [hbm((TOK, 2), jnp.int32), hbm((EXPERTS, TAGGED, 128), BF)],
        "dispatch_grads",
        3,
        scratch=[pltpu.VMEM((EXPERTS * PLAIN, 128), F32), pltpu.VMEM((SLOTS, D), F32)],
        unread=[after],
    )


def heads_of(parts, which):
    return jnp.concatenate([x[which * TOK : (which + 1) * TOK, :] for x in parts], axis=0)


def attend_body(*refs):
    parts, outs, saved = refs[:CTX], refs[CTX : 2 * CTX], refs[2 * CTX]
    q, k, v = heads_of(parts, 0), heads_of(parts, 1), heads_of(parts, 2)
    scores = dot_cols(q, k) * SCORE_SCALE
    top = jnp.max(scores, axis=1, keepdims=True)
    weights = jnp.exp(scores - top)
    total = jnp.sum(weights, axis=1, keepdims=True)
    mixed = (dot(weights.astype(BF), v) / total).astype(BF)
    for i, x in enumerate((q, k, v, mixed)):
        saved[i] = x
    for s, out in enumerate(outs):
        out[...] = mixed[s * TOK : (s + 1) * TOK]


ONE_HEAD = pl.BlockSpec((TOK, HDIM), lambda h: (0, h))
THREE_HEADS = pl.BlockSpec((3 * TOK, HDIM), lambda h: (0, h))
SAVED = pl.BlockSpec((4, CTX * TOK, HDIM), lambda h: (0, 0, h))


def attend(parts):
    return pl.pallas_call(
        attend_body,
        grid=(WIDE // HDIM,),
        in_specs=[THREE_HEADS] * CTX,
        out_specs=[ONE_HEAD] * CTX + [SAVED],
        out_shape=[hbm((TOK, WIDE), BF)] * CTX + [hbm((4, CTX * TOK, WIDE), BF)],
        compiler_params=params(),
        cost_estimate=cost(10),
        name="attend_forward",
    )(*parts)


def attend_back_body(saved, *refs):
    grads, outs = refs[:CTX], refs[CTX:]
    q, k, v, o = (saved[i] for i in range(4))
    g = heads_of(grads, 0)
    scores = dot_cols(q, k) * SCORE_SCALE
    top = jnp.max(scores, axis=1, keepdims=True)
    total = jnp.sum(jnp.exp(scores - top), axis=1, keepdims=True)
    prob = jnp.exp(scores - (top + jnp.log(total)))
    row_dot = jnp.sum(g.astype(F32) * o.astype(F32), axis=1, keepdims=True)
    score_grad = (prob * (dot_cols(g, v) - row_dot)).astype(BF)
    dq = (dot(score_grad, k) * SCORE_SCALE).astype(BF)
    dk = (dot_rows(score_grad, q) * SCORE_SCALE).astype(BF)
    dv = dot_rows(prob.astype(BF), g).astype(BF)
    for s, out in enumerate(outs):
        rows = slice(s * TOK, (s + 1) * TOK)
        out[0:TOK] = dq[rows]
        out[TOK : 2 * TOK] = dk[rows]
        out[2 * TOK :] = dv[rows]


def attend_back(saved, grads):
    return pl.pallas_call(
        attend_back_body,
        grid=(WIDE // HDIM,),
        in_specs=[SAVED] + [ONE_HEAD] * CTX,
        out_specs=[THREE_HEADS] * CTX,
        out_shape=[hbm((3 * TOK, WIDE), BF)] * CTX,
        compiler_params=params(),
        cost_estimate=cost(100),
        name="attend_backward",
    )(saved, *grads)


def norm_body(
    group, attn_0, attn_1, attn_2, attn_3, resid, scale, shift, router, ids, place,
    send, kept, gate, inverse, hidden, stage, picked,
):
    square = jnp.zeros((TOK, 1), F32)
    for s, attn in enumerate((attn_0, attn_1, attn_2, attn_3)):
        cols = group_cols(group, s)
        part = resid[:, cols].astype(F32) + attn[...].astype(F32)
        hidden[:, cols] = part
        square = square + jnp.sum(part * part, axis=1, keepdims=True)
    inv = lax.rsqrt(square / D + NORM_EPSILON)
    normed_mod = (hidden[...] * inv * (1.0 + scale[...]) + shift[...]).astype(BF)
    kept[...] = normed_mod
    inverse[...] = jnp.broadcast_to(inv, (TOK, 128))
    pick = (one_hot(place[:, 0:1], SLOTS) + one_hot(place[:, 1:2], SLOTS)).astype(BF)
    picked[...] = dot_rows(pick, normed_mod)
    ref_to_blocks(picked, stage)
    store_blocks(stage, send)
    logits = dot_cols(normed_mod, router[...])
    hot = one_hot(ids[:, 0:1], EXPERTS) - one_hot(ids[:, 1:2], EXPERTS)
    margin = jnp.sum(logits * hot, axis=1, keepdims=True)
    gate[...] = jnp.broadcast_to(jax.nn.sigmoid(margin), (TOK, 128))


def send_rows(group, attn, resid, scale, shift, router, ids, place):
    return staged(
        norm_body,
        [group],
        [*attn, resid, scale, shift, router, ids, place],
        [
            hbm((EXPERTS, PLAIN, 128), BF),
            hbm((TOK, D), BF),
            hbm((TOK, 128), F32),
            hbm((TOK, 128), F32),
        ],
        "norm_dispatch",
        3,
        scratch=[
            pltpu.VMEM((TOK, D), F32),
            pltpu.VMEM((EXPERTS * PLAIN, 128), F32),
            pltpu.VMEM((SLOTS, D), F32),
        ],
    )


def gelu_terms(pre):
    square = pre * pre
    turn = jnp.tanh(GELU_C * (pre + 0.044715 * pre * square))
    return square, turn


def forward_body(
    arrived, arrived_grads, w_in, w_out, router, own,
    rows, row_grads, pre_out, y_send,
    stage, y_sum, branch_grad,
):
    step = pl.program_id(0)

    @pl.when(step == 0)
    def _():
        from_blocks(arrived_grads.at[:, 0:PLAIN, :], stage, branch_grad, PLAIN)
        from_blocks(arrived, stage, rows, PLAIN)
        partner_table = arrived_grads[:, PLAIN : PLAIN + 16, :].astype(F32)[:, 0, :]
        partner = jnp.concatenate(
            [partner_table[:, s : s + 1] for s in range(CAP)], axis=0
        ).astype(jnp.int32)
        logits = dot_cols(rows[...], router[...])
        margin = jnp.sum(logits * (own[...] - one_hot(partner, EXPERTS)), axis=1, keepdims=True)
        row_grads[...] = (jax.nn.sigmoid(margin) * branch_grad[...].astype(F32)).astype(BF)
        y_sum[...] = jnp.zeros_like(y_sum)

    pre = dot(rows[...], w_in[0])
    pre_out[0] = pre
    _, turn = gelu_terms(pre)
    act = (0.5 * pre * (1.0 + turn)).astype(BF)
    y_sum[...] += dot(act, w_out[0]).astype(BF).astype(F32)

    @pl.when(step == CTX - 1)
    def _():
        ref_to_blocks(y_sum, stage)
        store_blocks(stage, y_send)


def whole(*dims):
    return pl.BlockSpec(dims, lambda b: (0,) * len(dims))


def of_block(*dims):
    return pl.BlockSpec((1,) + dims, lambda b: (b,) + (0,) * len(dims))


def experts_forward(arrived, arrived_grads, w_in, w_out, router, own):
    return pl.pallas_call(
        forward_body,
        grid=(CTX,),
        in_specs=[
            whole(EXPERTS, PLAIN, 128),
            whole(EXPERTS, TAGGED, 128),
            of_block(D, FF_BLOCK),
            of_block(FF_BLOCK, D),
            whole(EXPERTS, D),
            whole(1, EXPERTS),
        ],
        out_specs=[
            whole(SLOTS, D),
            whole(SLOTS, D),
            of_block(SLOTS, FF_BLOCK),
            whole(EXPERTS, PLAIN, 128),
        ],
        out_shape=[
            hbm((SLOTS, D), BF),
            hbm((SLOTS, D), BF),
            hbm((CTX, SLOTS, FF_BLOCK), F32),
            hbm((EXPERTS, PLAIN, 128), BF),
        ],
        scratch_shapes=[
            pltpu.VMEM((EXPERTS * PLAIN, 128), F32),
            pltpu.VMEM((SLOTS, D), F32),
            pltpu.VMEM((SLOTS, D), BF),
        ],
        compiler_params=params(60),
        cost_estimate=cost(10),
        name="expert_forward",
    )(arrived, arrived_grads, w_in, w_out, router, own)


def backward_body(rows, row_grads, pre_in, w_in, w_out, in_send, out_send, part_send, stage, part_sum):
    step = pl.program_id(0)

    @pl.when(step == 0)
    def _():
        part_sum[...] = jnp.zeros_like(part_sum)

    pre = pre_in[0]
    square, turn = gelu_terms(pre)
    act = (0.5 * pre * (1.0 + turn)).astype(BF)
    slope = 0.5 * (1.0 + turn) + 0.5 * pre * (1.0 - turn * turn) * (
        GELU_C * (1.0 + 3.0 * 0.044715 * square)
    )
    pre_grad = (dot_cols(row_grads[...], w_out[0]) * slope).astype(BF)
    part_sum[...] += dot_cols(pre_grad, w_in[0]).astype(BF).astype(F32)
    in_send[0] = dot_rows(rows[...], pre_grad).astype(BF)
    out_send[0] = dot_rows(act, row_grads[...]).astype(BF)

    @pl.when(step == CTX - 1)
    def _():
        ref_to_blocks(part_sum, stage)
        store_blocks(stage, part_send.at[:, 0:PLAIN, :])
        part_send[:, PLAIN:, :] = jnp.zeros((EXPERTS, CHUNKS, 128), BF)


def experts_backward(rows, row_grads, pre, w_in, w_out):
    return pl.pallas_call(
        backward_body,
        grid=(CTX,),
        in_specs=[
            whole(SLOTS, D),
            whole(SLOTS, D),
            of_block(SLOTS, FF_BLOCK),
            of_block(D, FF_BLOCK),
            of_block(FF_BLOCK, D),
        ],
        out_specs=[of_block(D, FF_BLOCK), of_block(FF_BLOCK, D), whole(EXPERTS, TAGGED, 128)],
        out_shape=[
            hbm((CTX, D, FF_BLOCK), BF),
            hbm((CTX, FF_BLOCK, D), BF),
            hbm((EXPERTS, TAGGED, 128), BF),
        ],
        scratch_shapes=[pltpu.VMEM((EXPERTS * PLAIN, 128), F32), pltpu.VMEM((SLOTS, D), F32)],
        compiler_params=params(60),
        cost_estimate=cost(15),
        name="expert_backward",
    )(rows, row_grads, pre, w_in, w_out)


def one_hots(ids):
    return one_hot(ids[:, 0:1], EXPERTS), one_hot(ids[:, 1:2], EXPERTS)


def resid_body(
    group, arrived, attn_0, attn_1, attn_2, attn_3, resid, grad_out, scale, router, place, logit_grad, inverse,
    resid_grad, router_column, send_0, send_1, send_2, send_3,
    stage, back, normed, lifted,
):
    from_blocks(arrived.at[:, 0:PLAIN, :], stage, back, PLAIN)
    router_column[...] = jnp.sum(arrived[:, PLAIN:TAGGED, :].astype(F32), axis=0)
    pick = (one_hot(place[:, 0:1], SLOTS) + one_hot(place[:, 1:2], SLOTS)).astype(BF)
    input_grad = dot(pick, back[...]) + dot(logit_grad[...], router[...])
    inv = inverse[:, 0:1]
    lifted[...] = input_grad * (1.0 + scale[...])
    mean = jnp.zeros((TOK, 1), F32)
    for s, attn in enumerate((attn_0, attn_1, attn_2, attn_3)):
        cols = group_cols(group, s)
        part = (resid[:, cols].astype(F32) + attn[...].astype(F32)) * inv
        normed[:, cols] = part
        mean = mean + jnp.sum(part * lifted[:, cols], axis=1, keepdims=True)
    mean = mean / D
    for s, send in enumerate((send_0, send_1, send_2, send_3)):
        cols = group_cols(group, s)
        part = grad_out[:, cols].astype(F32) + inv * (lifted[:, cols] - normed[:, cols] * mean)
        low_part = part.astype(BF)
        resid_grad[:, cols] = low_part
        send[...] = low_part


def resid_back(group, arrived, attn, resid, grad_out, scale, router, place, logit_grad, inverse):
    return staged(
        resid_body,
        [group],
        [arrived, *attn, resid, grad_out, scale, router, place, logit_grad, inverse],
        [hbm((TOK, D), BF), hbm((CHUNKS, 128), F32)] + [hbm((TOK, WIDE), BF)] * CTX,
        "resid_backward",
        30,
        scratch=[
            pltpu.VMEM((EXPERTS * PLAIN, 128), F32),
            pltpu.VMEM((SLOTS, D), BF),
            pltpu.VMEM((TOK, D), F32),
            pltpu.VMEM((TOK, D), F32),
        ],
        mib=60,
    )


def mixed_body(
    group, arrived, attn_0, attn_1, attn_2, attn_3, resid, grad_out, mod_gate, ids, place, gate, kept,
    out, logit_out, part_send,
    stage, back, branch, terms_blocks, sent_terms, sent,
):
    from_blocks(arrived, stage, back, PLAIN)
    gate_one = gate[:, 0:1]
    branch_grad = mod_gate[...] * grad_out[...].astype(F32)
    result_one = dot(one_hot(place[:, 0:1], SLOTS).astype(BF), back[...])
    pull = jnp.sum(branch_grad * result_one, axis=1, keepdims=True)
    result_two = dot(one_hot(place[:, 1:2], SLOTS).astype(BF), back[...])
    pull = pull - jnp.sum(branch_grad * result_two, axis=1, keepdims=True)
    first_hot, second_hot = one_hots(ids)
    tilt = pull * gate_one * (1.0 - gate_one)
    logit_grad = (tilt * (first_hot - second_hot)).astype(BF)
    logit_out[...] = logit_grad
    terms = dot_rows(logit_grad, kept[...])
    for c in range(CHUNKS):
        terms_blocks[pl.ds(c, EXPERTS, stride=CHUNKS), :] = terms[:, c * 128 : (c + 1) * 128]
    sent_terms[...] = terms_blocks[...].reshape(EXPERTS, CHUNKS, 128).astype(BF)
    copy = pltpu.make_async_copy(sent_terms, part_send.at[:, PLAIN:TAGGED, :], sent.at[0])
    copy.start()
    branch[...] = mod_gate[...] * (gate_one * result_one + (1.0 - gate_one) * result_two)
    for s, attn in enumerate((attn_0, attn_1, attn_2, attn_3)):
        cols = group_cols(group, s)
        hidden = resid[:, cols].astype(F32) + attn[...].astype(F32)
        out[:, cols] = (hidden + branch[:, cols]).astype(BF)
    copy.wait()


def mix(group, arrived, attn, resid, grad_out, mod_gate, ids, place, gate, kept, part_rows):
    return staged(
        mixed_body,
        [group],
        [arrived, *attn, resid, grad_out, mod_gate, ids, place, gate, kept],
        [hbm((TOK, D), BF), hbm((TOK, EXPERTS), BF)],
        "mixed_output",
        5,
        scratch=[
            pltpu.VMEM((EXPERTS * PLAIN, 128), F32),
            pltpu.VMEM((SLOTS, D), BF),
            pltpu.VMEM((TOK, D), F32),
            pltpu.VMEM((EXPERTS * CHUNKS, 128), F32),
            pltpu.VMEM((EXPERTS, CHUNKS, 128), BF),
            pltpu.SemaphoreType.DMA((1,)),
        ],
        mib=60,
        carried=part_rows,
    )


def order_body(blocks, out, stage):
    stage[...] = blocks[...].reshape(EXPERTS * CHUNKS, 128)
    for c in range(CHUNKS):
        out[:, c * 128 : (c + 1) * 128] = stage[pl.ds(c, EXPERTS, stride=CHUNKS), :]


def order_router(blocks):
    return staged(
        order_body,
        [],
        [blocks],
        hbm((EXPERTS, D), F32),
        "order_router",
        2,
        scratch=[pltpu.VMEM((EXPERTS * CHUNKS, 128), F32)],
    )


def swap(x):
    return lax.all_to_all(x, "expert", split_axis=0, concat_axis=0, tiled=True)


def shift(x, axis, count, step):
    return lax.ppermute(x, axis, [(i, (i + step) % count) for i in range(count)])


def around(parts, sign):
    return [parts[0]] + [shift(parts[s], "ctx", CTX, sign * s) for s in range(1, CTX)]


def local(
    resid, queries, keys, values, mod_scale, mod_shift, mod_gate, router, w_in, w_out, expert_ids, grad_out
):
    group = lax.axis_index("ctx").astype(jnp.int32)[None]
    expert = lax.axis_index("expert").astype(jnp.int32)
    own = (jnp.arange(EXPERTS, dtype=jnp.int32) == expert).astype(F32)[None, :]
    router_rows = router.T
    packed = pack(group, queries, keys, values)
    heads = around(packed, 1)
    place, grads = send_grads(grad_out, mod_gate, expert_ids, packed[0])
    arrived_grads = swap(grads)
    full_in = lax.all_gather(w_in, "ctx", axis=0, tiled=True)
    full_out = lax.all_gather(w_out, "ctx", axis=0, tiled=True)
    *attn_heads, saved = attend(heads)
    attn = around(attn_heads, -1)
    rows, kept, gate, inverse = send_rows(
        group, attn, resid, mod_scale, mod_shift, router_rows, expert_ids, place
    )
    arrived = swap(rows)
    flat_rows, flat_grads, pre_act, y_rows = experts_forward(
        arrived, arrived_grads, full_in, full_out, router_rows, own
    )
    outputs = swap(y_rows)
    in_terms, out_terms, part_rows = experts_backward(flat_rows, flat_grads, pre_act, full_in, full_out)
    in_terms, out_terms, _ = lax.optimization_barrier((in_terms, out_terms, outputs))
    grad_w_in, grad_w_out = (
        lax.psum_scatter(x, "ctx", scatter_dimension=0, tiled=True) for x in (in_terms, out_terms)
    )
    mixed_out, logit_grad, part_rows = mix(
        group, outputs, attn, resid, grad_out, mod_gate, expert_ids, place, gate, kept, part_rows
    )
    parts = swap(part_rows)
    resid_grad, router_column, *head_grads = resid_back(
        group, parts, attn, resid, grad_out, mod_scale, router_rows, place, logit_grad, inverse
    )
    attn_grads = around(head_grads, 1)
    head_terms = attend_back(saved, attn_grads)
    head_sums = around(head_terms, -1)
    router_column, *_ = lax.optimization_barrier((router_column, *attn_grads[1:]))
    *columns, _ = lax.optimization_barrier((*around([router_column] * CTX, 1), head_terms[0]))
    router_column = columns[0] + columns[1] + columns[2] + columns[3]
    grad_router = order_router(
        swap(jnp.broadcast_to(router_column, (EXPERTS, CHUNKS, 128)))
    ).T
    grad_queries, grad_keys, grad_values = unpack(group, head_sums)
    return (
        mixed_out,
        resid_grad,
        grad_queries,
        grad_keys,
        grad_values,
        grad_w_in,
        grad_w_out,
        grad_router,
    )


def solution(mesh):
    tokens = P(("expert", "ctx"), None)
    clip = P("expert", None)
    return jax.shard_map(
        local,
        mesh=mesh,
        in_specs=(
            tokens, tokens, tokens, tokens, clip, clip, clip, P(),
            P("expert", None, "ctx"), P("expert", "ctx", None), tokens, tokens,
        ),
        out_specs=(
            tokens, tokens, tokens, tokens, tokens,
            P("expert", None, "ctx"), P("expert", "ctx", None), P(),
        ),
        check_vma=False,
    )
```

profile of v0, /device:TPU:1, one launch (start us, length us, event | category | flops | bytes accessed | tf_op | source)
XLA Modules:
  0.0 328.8 jit_solution(1848265499609390538)
XLA Ops:
  8.0 0.7 all-gather.5.cloned.1.call-update
  8.9 1.4 pack_heads.1
  10.4 1.0 copy-done.4
  11.4 4.0 %dispatch_grads.1 = (s32[128,2]{1,0:T(8,128)}, bf16[64,96,128]{2,1,0:T(8,128)(2,1)}) custom-call(bf16[128,2048]{1,0:T(8,128)(2,1)S(1)} %copy-done.1, f32[1,2048]{1,0:T(1,128)S(1)} %copy-done.17, s32[128,2]{1,0:T(8,128)S(1)} %copy.25.refs_2_.refs_9_, bf16[384,512]{1,0:T(8,128)(2,1)S(1)} %copy-done.4), custom_call_target="tpu_custom_call" | custom-call | bytes 9000000 | tf_op jit(solution)/shard_map/dispatch_grads/pallas_call | solution.py:90
  15.4 13.5 %all-to-all-start.1 = ((bf16[64,96,128]{2,1,0:T(8,128)(2,1)}), bf16[64,96,128]{2,1,0:T(8,128)(2,1)}, u32[]{:S(2)}, u32[]{:S(2)}) async-start(bf16[64,96,128]{2,1,0:T(8,128)(2,1)} %get-tuple-element.63), calls=%async_computation.1 | async-start | bytes 3145728 | tf_op jit(solution)/shard_map/all_to_all | solution.py:584
  29.0 1.3 collective-permute-start
  30.3 2.4 collective-permute-start.1
  32.7 1.2 collective-permute-start.2
  33.9 15.7 %collective-permute-done.refs_1_ = bf16[384,512]{1,0:T(8,128)(2,1)S(1)} collective-permute-done((bf16[384,512]{1,0:T(8,128)(2,1)S(1)}, bf16[384,512]{1,0:T(8,128)(2,1)S(1)}, u32[]{:S(2)}, u32[]{:S(2)}) %collective-permute-start) | collective-permute-done | bytes 393248 | tf_op jit(solution)/shard_map/ppermute | solution.py:588
  49.6 17.8 %collective-permute-done.1.refs_2_ = bf16[384,512]{1,0:T(8,128)(2,1)S(1)} collective-permute-done((bf16[384,512]{1,0:T(8,128)(2,1)S(1)}, bf16[384,512]{1,0:T(8,128)(2,1)S(1)}, u32[]{:S(2)}, u32[]{:S(2)}) %collective-permute-start.1) | collective-permute-done | bytes 393248 | tf_op jit(solution)/shard_map/ppermute | solution.py:588
  67.4 4.6 %attend_forward.1 = (bf16[128,512]{1,0:T(8,128)(2,1)}, bf16[128,512]{1,0:T(8,128)(2,1)}, bf16[128,512]{1,0:T(8,128)(2,1)}, bf16[128,512]{1,0:T(8,128)(2,1)}, bf16[4,512,512]{2,1,0:T(8,128)(2,1)}) custom-call(bf16[384,512]{1,0:T(8,128)(2,1)S(1)} %copy-done.5, bf16[384,512]{1,0:T(8,128)(2,1)S(1)} %collective-permute-done.refs_1_, ...), custom_call_target="tpu_custom_call" | custom-call | bytes 30000000 | tf_op jit(solution)/shard_map/attend_forward/pallas_call | solution.py:246
  72.2 2.0 collective-permute-start.4
  74.2 0.9 collective-permute-start.5
  75.1 5.0 %collective-permute-done.3.refs_2_.refs_3_ = bf16[128,512]{1,0:T(8,128)(2,1)S(1)} collective-permute-done((bf16[128,512]{1,0:T(8,128)(2,1)}, bf16[128,512]{1,0:T(8,128)(2,1)S(1)}, u32[]{:S(2)}, u32[]{:S(2)}) %collective-permute-start.3) | collective-permute-done | bytes 131104 | tf_op jit(solution)/shard_map/ppermute | solution.py:588
  80.1 1.4 collective-permute-done.4.refs_3_.refs_4_
  81.4 4.4 %collective-permute-done.5.refs_4_.refs_5_ = bf16[128,512]{1,0:T(8,128)(2,1)S(1)} collective-permute-done((bf16[128,512]{1,0:T(8,128)(2,1)}, bf16[128,512]{1,0:T(8,128)(2,1)S(1)}, u32[]{:S(2)}, u32[]{:S(2)}) %collective-permute-start.5) | collective-permute-done | bytes 131104 | tf_op jit(solution)/shard_map/ppermute | solution.py:588
  85.9 0.9 copy-done.6
  86.8 4.7 %norm_dispatch.1 = (bf16[64,80,128]{2,1,0:T(8,128)(2,1)}, bf16[128,2048]{1,0:T(8,128)(2,1)}, f32[128,128]{1,0:T(8,128)}, f32[128,128]{1,0:T(8,128)}) custom-call(s32[1]{0:T(128)} %bitcast.refs_0_, bf16[128,512]{1,0:T(8,128)(2,1)S(1)} %copy-done.6, bf16[128,512]{1,0:T(8,128)(2,1)S(1)} %collective-permute-done.3.refs_2_.refs_3_, ...), custom_call_target="tpu_custom_call" | custom-call | bytes 9000000 | tf_op jit(solution)/shard_map/norm_dispatch/pallas_call | solution.py:90
  91.6 11.3 %all-to-all-start = ((bf16[64,80,128]{2,1,0:T(8,128)(2,1)}), bf16[64,80,128]{2,1,0:T(8,128)(2,1)S(1)}, u32[]{:S(2)}, u32[]{:S(2)}) async-start(bf16[64,80,128]{2,1,0:T(8,128)(2,1)} %get-tuple-element.62), calls=%async_computation | async-start | bytes 2621440 | tf_op jit(solution)/shard_map/all_to_all | solution.py:584
  103.4 33.6 %all-to-all-done.arrived = bf16[64,80,128]{2,1,0:T(8,128)(2,1)S(1)} async-done(((bf16[64,80,128]{2,1,0:T(8,128)(2,1)}), bf16[64,80,128]{2,1,0:T(8,128)(2,1)S(1)}, u32[]{:S(2)}, u32[]{:S(2)}) %all-to-all-start) | async-done | bytes 1310752 | tf_op jit(solution)/shard_map/all_to_all | solution.py:584
  137.1 2.5 all-gather.5.cloned.1.call-done.w_out
  139.6 15.4 %expert_forward.1 = (bf16[320,2048]{1,0:T(8,128)(2,1)}, bf16[320,2048]{1,0:T(8,128)(2,1)}, f32[4,320,256]{2,1,0:T(8,128)}, bf16[64,80,128]{2,1,0:T(8,128)(2,1)}) custom-call(bf16[64,80,128]{2,1,0:T(8,128)(2,1)} %copy-done.21, bf16[64,96,128]{2,1,0:T(8,128)(2,1)} %all-to-all-done.1.arrived_grads, bf16[4,2048,256]{2,1,0:T(8,128)(2,1)} %all-gather.3.cloned.1.call-done.w_in, ...), custom_call_target="tpu_custom_call" | custom-call | bytes 30000000 | tf_op jit(solution)/shard_map/expert_forward/pallas_call | solution.py:383
  155.0 10.7 %all-to-all-start.2 = ((bf16[64,80,128]{2,1,0:T(8,128)(2,1)}), bf16[64,80,128]{2,1,0:T(8,128)(2,1)S(1)}, u32[]{:S(2)}, u32[]{:S(2)}) async-start(bf16[64,80,128]{2,1,0:T(8,128)(2,1)} %get-tuple-element.64), calls=%async_computation.2 | async-start | bytes 2621440 | tf_op jit(solution)/shard_map/all_to_all | solution.py:584
  165.7 17.4 %expert_backward.1 = (bf16[4,2048,256]{2,1,0:T(8,128)(2,1)}, bf16[4,256,2048]{2,1,0:T(8,128)(2,1)}, bf16[64,96,128]{2,1,0:T(8,128)(2,1)}) custom-call(bf16[320,2048]{1,0:T(8,128)(2,1)} %get-tuple-element.67.rows, bf16[320,2048]{1,0:T(8,128)(2,1)} %get-tuple-element.68.row_grads, f32[4,320,256]{2,1,0:T(8,128)} %get-tuple-element.69.pre_in, ...), custom_call_target="tpu_custom_call" | custom-call | bytes 45000000 | tf_op jit(solution)/shard_map/expert_backward/pallas_call | solution.py:443
  183.2 16.7 %all-to-all-done.2.refs_1_ = bf16[64,80,128]{2,1,0:T(8,128)(2,1)S(1)} async-done(((bf16[64,80,128]{2,1,0:T(8,128)(2,1)}), bf16[64,80,128]{2,1,0:T(8,128)(2,1)S(1)}, u32[]{:S(2)}, u32[]{:S(2)}) %all-to-all-start.2) | async-done | bytes 1310752 | tf_op jit(solution)/shard_map/all_to_all | solution.py:584
  199.9 1.0 copy-done.20
  201.5 6.4 %mixed_output.1 = (bf16[128,2048]{1,0:T(8,128)(2,1)}, bf16[128,64]{1,0:T(8,128)(2,1)}, bf16[64,96,128]{2,1,0:T(8,128)(2,1)}) custom-call(s32[1]{0:T(128)} %bitcast.refs_0_, bf16[64,80,128]{2,1,0:T(8,128)(2,1)} %copy-done.20, bf16[128,512]{1,0:T(8,128)(2,1)} %get-tuple-element.57.refs_1_.refs_2_, ...), custom_call_target="tpu_custom_call", output_to_operand_aliasing={{2}: (13, {})} | custom-call | bytes 15000000 | tf_op jit(solution)/shard_map/mixed_output/pallas_call | solution.py:90
  207.9 46.1 %all_to_all.25.refs_1_ = bf16[64,96,128]{2,1,0:T(8,128)(2,1)} all-to-all(bf16[64,96,128]{2,1,0:T(8,128)(2,1)} %get-tuple-element.72), channel_id=1, replica_groups=mesh['expert'=64,'ctx'=4] {'expert'}, dimensions={0} | all-to-all | bytes 3145728 | tf_op jit(solution)/shard_map/all_to_all | solution.py:584
  253.9 5.1 %resid_backward.1 = (bf16[128,2048]{1,0:T(8,128)(2,1)}, f32[16,128]{1,0:T(8,128)}, bf16[128,512]{1,0:T(8,128)(2,1)}, bf16[128,512]{1,0:T(8,128)(2,1)}, bf16[128,...) custom-call(s32[1]{0:T(128)} %bitcast.refs_0_, bf16[64,96,128]{2,1,0:T(8,128)(2,1)} %all_to_all.25.refs_1_, ...), custom_call_target="tpu_custom_call" | custom-call | bytes 90000000 | tf_op jit(solution)/shard_map/resid_backward/pallas_call | solution.py:90
  259.7 1.5 collective-permute-start.7
  261.2 1.8 collective-permute-start.8
  263.0 5.8 %collective-permute-done.6.refs_1_ = bf16[128,512]{1,0:T(8,128)(2,1)S(1)} collective-permute-done((bf16[128,512]{1,0:T(8,128)(2,1)}, bf16[128,512]{1,0:T(8,128)(2,1)S(1)}, u32[]{:S(2)}, u32[]{:S(2)}) %collective-permute-start.6) | collective-permute-done | bytes 131104 | tf_op jit(solution)/shard_map/ppermute | solution.py:588
  268.8 4.0 %collective-permute-done.7.refs_2_ = bf16[128,512]{1,0:T(8,128)(2,1)S(1)} collective-permute-done((bf16[128,512]{1,0:T(8,128)(2,1)}, bf16[128,512]{1,0:T(8,128)(2,1)S(1)}, u32[]{:S(2)}, u32[]{:S(2)}) %collective-permute-start.7) | collective-permute-done | bytes 131104 | tf_op jit(solution)/shard_map/ppermute | solution.py:588
  272.8 2.0 collective-permute-done.8.refs_3_
  275.1 1.4 collective-permute-start.13
  276.6 0.9 collective-permute-start.12
  277.4 0.9 copy-done.16
  278.3 6.7 %attend_backward.1 = (bf16[384,512]{1,0:T(8,128)(2,1)}, bf16[384,512]{1,0:T(8,128)(2,1)}, bf16[384,512]{1,0:T(8,128)(2,1)}, bf16[384,512]{1,0:T(8,128)(2,1)}) custom-call(bf16[4,512,512]{2,1,0:T(8,128)(2,1)S(1)} %copy-done.3, bf16[128,512]{1,0:T(8,128)(2,1)S(1)} %copy-done.16, bf16[128,512]{1,0:T(8,128)(2,1)S(1)} %collective-permute-done.6.refs_1_, ...), custom_call_target="tpu_custom_call" | custom-call | bytes 300000000 | tf_op jit(solution)/shard_map/attend_backward/pallas_call | solution.py:279
  285.1 0.8 broadcast_in_dim.8
  286.0 6.9 %all-to-all-start.4 = ((f32[64,16,128]{2,1,0:T(8,128)}), f32[64,16,128]{2,1,0:T(8,128)S(1)}, u32[]{:S(2)}, u32[]{:S(2)}) async-start(f32[64,16,128]{2,1,0:T(8,128)} %broadcast_in_dim.8), calls=%async_computation.6 | async-start | bytes 1048576 | tf_op jit(solution)/shard_map/all_to_all | solution.py:584
  292.9 1.7 collective-permute-start.9
  294.6 1.3 collective-permute-start.10
  295.9 0.8 collective-permute-start.11
  296.7 12.8 %collective-permute-done.9.refs_2_ = bf16[384,512]{1,0:T(8,128)(2,1)S(1)} collective-permute-done((bf16[384,512]{1,0:T(8,128)(2,1)S(1)}, bf16[384,512]{1,0:T(8,128)(2,1)S(1)}, u32[]{:S(2)}, u32[]{:S(2)}) %collective-permute-start.9) | collective-permute-done | bytes 393248 | tf_op jit(solution)/shard_map/ppermute | solution.py:588
  309.4 1.0 collective-permute-done.10.refs_3_
  310.4 8.7 %collective-permute-done.11.refs_4_ = bf16[384,512]{1,0:T(8,128)(2,1)S(1)} collective-permute-done((bf16[384,512]{1,0:T(8,128)(2,1)S(1)}, bf16[384,512]{1,0:T(8,128)(2,1)S(1)}, u32[]{:S(2)}, u32[]{:S(2)}) %collective-permute-start.11) | collective-permute-done | bytes 393248 | tf_op jit(solution)/shard_map/ppermute | solution.py:588
  319.1 2.0 unpack_heads.1
  321.1 1.0 order_router.1
  (78 shorter events, 3.3 us)
Async XLA Ops:
  7.2 1.7 copy-start.14
  7.2 1.7 copy-start.13
  7.2 1.7 copy-start.12
  7.2 129.9 %all-gather.3.cloned.1.call-start = ((), (), s32[]{:S(2)}) async-start(), calls=%async_computation.7 | async-start | bytes 5242880 | tf_op jit(solution)/shard_map/all_gather | solution.py:606
  7.9 2.4 copy-start.1
  8.0 2.4 copy-start.17
  8.0 131.6 %all-gather.5.cloned.1.call-start = ((), (), s32[]{:S(2)}) async-start(), calls=%async_computation.8 | async-start | bytes 5242880 | tf_op jit(solution)/shard_map/all_gather | solution.py:607
  8.8 77.0 %copy-start.10 = (s32[128,2]{1,0:T(8,128)}, s32[128,2]{1,0:T(8,128)S(1)}, u32[]{:S(2)}) copy-start(s32[128,2]{1,0:T(8,128)S(1)} %copy.25.refs_2_.refs_9_) | copy-start | bytes 3076
  15.4 13.6 %copy-start.29 = (bf16[384,512]{1,0:T(8,128)(2,1)S(1)}, bf16[384,512]{1,0:T(8,128)(2,1)}, u32[]{:S(2)}) copy-start(bf16[384,512]{1,0:T(8,128)(2,1)} %get-tuple-element.54) | copy-start | bytes 1179652
  15.4 14.9 %copy-start.28 = (bf16[384,512]{1,0:T(8,128)(2,1)S(1)}, bf16[384,512]{1,0:T(8,128)(2,1)}, u32[]{:S(2)}) copy-start(bf16[384,512]{1,0:T(8,128)(2,1)} %get-tuple-element.55) | copy-start | bytes 1179652
  15.4 17.3 %copy-start.27 = (bf16[384,512]{1,0:T(8,128)(2,1)S(1)}, bf16[384,512]{1,0:T(8,128)(2,1)}, u32[]{:S(2)}) copy-start(bf16[384,512]{1,0:T(8,128)(2,1)} %get-tuple-element.56) | copy-start | bytes 1179652
  15.4 52.0 %copy-start.5 = (bf16[384,512]{1,0:T(8,128)(2,1)S(1)}, bf16[384,512]{1,0:T(8,128)(2,1)}, u32[]{:S(2)}) copy-start(bf16[384,512]{1,0:T(8,128)(2,1)} %get-tuple-element.53.refs_0_.refs_3_) | copy-start | bytes 1179652
  15.4 76.1 %all-to-all-start.1 = ((bf16[64,96,128]{2,1,0:T(8,128)(2,1)}), bf16[64,96,128]{2,1,0:T(8,128)(2,1)}, u32[]{:S(2)}, u32[]{:S(2)}) async-start(bf16[64,96,128]{2,1,0:T(8,128)(2,1)} %get-tuple-element.63), calls=%async_computation.1 | async-start | bytes 3145728 | tf_op jit(solution)/shard_map/all_to_all | solution.py:584
  28.9 57.0 %copy-start = (bf16[128,2048]{1,0:T(8,128)(2,1)S(1)}, bf16[128,2048]{1,0:T(8,128)(2,1)}, u32[]{:S(2)}) copy-start(bf16[128,2048]{1,0:T(8,128)(2,1)} %refs_6_.5) | copy-start | bytes 1572868
  28.9 57.0 %copy-start.2 = (bf16[2048,64]{0,1:T(8,128)(2,1)S(1)}, bf16[2048,64]{0,1:T(8,128)(2,1)}, u32[]{:S(2)}) copy-start(bf16[2048,64]{0,1:T(8,128)(2,1)} %param.19) | copy-start | bytes 786436
  28.9 57.0 %copy-start.11 = (s32[128,2]{1,0:T(8,128)S(1)}, s32[128,2]{1,0:T(8,128)}, u32[]{:S(2)}) copy-start(s32[128,2]{1,0:T(8,128)} %get-tuple-element.61.refs_10_) | copy-start | bytes 3076
  28.9 57.0 %copy-start.18 = (f32[1,2048]{1,0:T(1,128)S(1)}, f32[1,2048]{1,0:T(1,128)}, u32[]{:S(2)}) copy-start(f32[1,2048]{1,0:T(1,128)} %refs_8_.3) | copy-start | bytes 24580
  28.9 57.0 %copy-start.19 = (f32[1,2048]{1,0:T(1,128)S(1)}, f32[1,2048]{1,0:T(1,128)}, u32[]{:S(2)}) copy-start(f32[1,2048]{1,0:T(1,128)} %refs_7_.3) | copy-start | bytes 24580
  29.0 20.6 %collective-permute-start = (bf16[384,512]{1,0:T(8,128)(2,1)S(1)}, bf16[384,512]{1,0:T(8,128)(2,1)S(1)}, u32[]{:S(2)}, u32[]{:S(2)}) collective-permute-start(bf16[384,512]{1,0:T(8,128)(2,1)S(1)} %copy-done.29), channel_id=1, source_target_pairs={{0,1},{1,2},{2,3},{3,0},{4,5},{5,6},{6,7},{7,4},{8,9},{9,10},{10,1... | collective-permute-start | bytes 1179656 | tf_op jit(solution)/shard_map/ppermute | solution.py:588
  30.3 37.1 %collective-permute-start.1 = (bf16[384,512]{1,0:T(8,128)(2,1)S(1)}, bf16[384,512]{1,0:T(8,128)(2,1)S(1)}, u32[]{:S(2)}, u32[]{:S(2)}) collective-permute-start(bf16[384,512]{1,0:T(8,128)(2,1)S(1)} %copy-done.28), channel_id=1, source_target_pairs={{0,2},{1,3},{2,0},{3,1},{4,6},{5,7},{6,4},{7,5},{8,10},{9,11},{10,... | collective-permute-start | bytes 1179656 | tf_op jit(solution)/shard_map/ppermute | solution.py:588
  32.7 34.7 %collective-permute-start.2 = (bf16[384,512]{1,0:T(8,128)(2,1)S(1)}, bf16[384,512]{1,0:T(8,128)(2,1)S(1)}, u32[]{:S(2)}, u32[]{:S(2)}) collective-permute-start(bf16[384,512]{1,0:T(8,128)(2,1)S(1)} %copy-done.27), channel_id=1, source_target_pairs={{0,3},{1,0},{2,1},{3,2},{4,7},{5,4},{6,5},{7,6},{8,11},{9,8},{10,9... | collective-permute-start | bytes 1179656 | tf_op jit(solution)/shard_map/ppermute | solution.py:588
  72.0 8.0 %collective-permute-start.3 = (bf16[128,512]{1,0:T(8,128)(2,1)}, bf16[128,512]{1,0:T(8,128)(2,1)S(1)}, u32[]{:S(2)}, u32[]{:S(2)}) collective-permute-start(bf16[128,512]{1,0:T(8,128)(2,1)} %get-tuple-element.58), channel_id=1, source_target_pairs={{0,3},{1,0},{2,1},{3,2},{4,7},{5,4},{6,5},{7,6},{8,11},{9,8},{10,9... | collective-permute-start | bytes 393224 | tf_op jit(solution)/shard_map/ppermute | solution.py:588
  72.2 9.2 %collective-permute-start.4 = (bf16[128,512]{1,0:T(8,128)(2,1)}, bf16[128,512]{1,0:T(8,128)(2,1)S(1)}, u32[]{:S(2)}, u32[]{:S(2)}) collective-permute-start(bf16[128,512]{1,0:T(8,128)(2,1)} %get-tuple-element.59), channel_id=1, source_target_pairs={{0,2},{1,3},{2,0},{3,1},{4,6},{5,7},{6,4},{7,5},{8,10},{9,11},{10,... | collective-permute-start | bytes 393224 | tf_op jit(solution)/shard_map/ppermute | solution.py:588
  74.2 11.6 %collective-permute-start.5 = (bf16[128,512]{1,0:T(8,128)(2,1)}, bf16[128,512]{1,0:T(8,128)(2,1)S(1)}, u32[]{:S(2)}, u32[]{:S(2)}) collective-permute-start(bf16[128,512]{1,0:T(8,128)(2,1)} %get-tuple-element.60), channel_id=1, source_target_pairs={{0,1},{1,2},{2,3},{3,0},{4,5},{5,6},{6,7},{7,4},{8,9},{9,10},{10,1... | collective-permute-start | bytes 393224 | tf_op jit(solution)/shard_map/ppermute | solution.py:588
  80.1 11.5 %copy-start.7 = (bf16[128,512]{1,0:T(8,128)(2,1)}, bf16[128,512]{1,0:T(8,128)(2,1)S(1)}, u32[]{:S(2)}) copy-start(bf16[128,512]{1,0:T(8,128)(2,1)S(1)} %collective-permute-done.3.refs_2_.refs_3_) | copy-start | bytes 393220
  81.4 10.1 %copy-start.8 = (bf16[128,512]{1,0:T(8,128)(2,1)}, bf16[128,512]{1,0:T(8,128)(2,1)S(1)}, u32[]{:S(2)}) copy-start(bf16[128,512]{1,0:T(8,128)(2,1)S(1)} %collective-permute-done.4.refs_3_.refs_4_) | copy-start | bytes 393220
  85.9 5.7 %copy-start.9 = (bf16[128,512]{1,0:T(8,128)(2,1)}, bf16[128,512]{1,0:T(8,128)(2,1)S(1)}, u32[]{:S(2)}) copy-start(bf16[128,512]{1,0:T(8,128)(2,1)S(1)} %collective-permute-done.5.refs_4_.refs_5_) | copy-start | bytes 393220
  91.6 45.5 %all-to-all-start = ((bf16[64,80,128]{2,1,0:T(8,128)(2,1)}), bf16[64,80,128]{2,1,0:T(8,128)(2,1)S(1)}, u32[]{:S(2)}, u32[]{:S(2)}) async-start(bf16[64,80,128]{2,1,0:T(8,128)(2,1)} %get-tuple-element.62), calls=%async_computation | async-start | bytes 2621440 | tf_op jit(solution)/shard_map/all_to_all | solution.py:584
  137.1 2.5 copy-start.21
  155.0 44.9 %all-to-all-start.2 = ((bf16[64,80,128]{2,1,0:T(8,128)(2,1)}), bf16[64,80,128]{2,1,0:T(8,128)(2,1)S(1)}, u32[]{:S(2)}, u32[]{:S(2)}) async-start(bf16[64,80,128]{2,1,0:T(8,128)(2,1)} %get-tuple-element.64), calls=%async_computation.2 | async-start | bytes 2621440 | tf_op jit(solution)/shard_map/all_to_all | solution.py:584
  165.7 156.5 %reduce-scatter.3.cloned.1.call-start = ((), (), s32[]{:S(2)}) async-start(), calls=%async_computation.9 | async-start | bytes 5242880 | tf_op jit(solution)/shard_map/reduce_scatter | solution.py:621
  200.9 121.3 %reduce-scatter.5.cloned.1.call-start = ((), (), s32[]{:S(2)}) async-start(), calls=%async_computation.10 | async-start | bytes 5242880 | tf_op jit(solution)/shard_map/reduce_scatter | solution.py:621
  253.9 23.5 %copy-start.3 = (bf16[4,512,512]{2,1,0:T(8,128)(2,1)S(1)}, bf16[4,512,512]{2,1,0:T(8,128)(2,1)}, u32[]{:S(2)}) copy-start(bf16[4,512,512]{2,1,0:T(8,128)(2,1)} %get-tuple-element.76.saved) | copy-start | bytes 6291460
  259.0 26.1 %copy-start.22 = (f32[16,128]{1,0:T(8,128)S(1)}, f32[16,128]{1,0:T(8,128)}, u32[]{:S(2)}) copy-start(f32[16,128]{1,0:T(8,128)} %get-tuple-element.94) | copy-start | bytes 24580
  259.1 9.8 %collective-permute-start.6 = (bf16[128,512]{1,0:T(8,128)(2,1)}, bf16[128,512]{1,0:T(8,128)(2,1)S(1)}, u32[]{:S(2)}, u32[]{:S(2)}) collective-permute-start(bf16[128,512]{1,0:T(8,128)(2,1)} %get-tuple-element.78), channel_id=1, source_target_pairs={{0,1},{1,2},{2,3},{3,0},{4,5},{5,6},{6,7},{7,4},{8,9},{9,10},{10,1... | collective-permute-start | bytes 393224 | tf_op jit(solution)/shard_map/ppermute | solution.py:588
  259.7 13.1 %collective-permute-start.7 = (bf16[128,512]{1,0:T(8,128)(2,1)}, bf16[128,512]{1,0:T(8,128)(2,1)S(1)}, u32[]{:S(2)}, u32[]{:S(2)}) collective-permute-start(bf16[128,512]{1,0:T(8,128)(2,1)} %get-tuple-element.79), channel_id=1, source_target_pairs={{0,2},{1,3},{2,0},{3,1},{4,6},{5,7},{6,4},{7,5},{8,10},{9,11},{10,... | collective-permute-start | bytes 393224 | tf_op jit(solution)/shard_map/ppermute | solution.py:588
  261.2 13.7 %collective-permute-start.8 = (bf16[128,512]{1,0:T(8,128)(2,1)}, bf16[128,512]{1,0:T(8,128)(2,1)S(1)}, u32[]{:S(2)}, u32[]{:S(2)}) collective-permute-start(bf16[128,512]{1,0:T(8,128)(2,1)} %get-tuple-element.80), channel_id=1, source_target_pairs={{0,3},{1,0},{2,1},{3,2},{4,7},{5,4},{6,5},{7,6},{8,11},{9,8},{10,9... | collective-permute-start | bytes 393224 | tf_op jit(solution)/shard_map/ppermute | solution.py:588
  274.9 10.2 %collective-permute-start.14 = (f32[16,128]{1,0:T(8,128)}, f32[16,128]{1,0:T(8,128)S(1)}, u32[]{:S(2)}, u32[]{:S(2)}) collective-permute-start(f32[16,128]{1,0:T(8,128)} %get-tuple-element.94), channel_id=1, source_target_pairs={{0,3},{1,0},{2,1},{3,2},{4,7},{5,4},{6,5},{7,6},{8,11},{9,8},{10,9... | collective-permute-start | bytes 24584 | tf_op jit(solution)/shard_map/ppermute | solution.py:588
  275.1 10.0 %collective-permute-start.13 = (f32[16,128]{1,0:T(8,128)}, f32[16,128]{1,0:T(8,128)S(1)}, u32[]{:S(2)}, u32[]{:S(2)}) collective-permute-start(f32[16,128]{1,0:T(8,128)} %get-tuple-element.94), channel_id=1, source_target_pairs={{0,2},{1,3},{2,0},{3,1},{4,6},{5,7},{6,4},{7,5},{8,10},{9,11},{10,... | collective-permute-start | bytes 24584 | tf_op jit(solution)/shard_map/ppermute | solution.py:588
  276.6 8.5 %collective-permute-start.12 = (f32[16,128]{1,0:T(8,128)}, f32[16,128]{1,0:T(8,128)S(1)}, u32[]{:S(2)}, u32[]{:S(2)}) collective-permute-start(f32[16,128]{1,0:T(8,128)} %get-tuple-element.94), channel_id=1, source_target_pairs={{0,1},{1,2},{2,3},{3,0},{4,5},{5,6},{6,7},{7,4},{8,9},{9,10},{10,1... | collective-permute-start | bytes 24584 | tf_op jit(solution)/shard_map/ppermute | solution.py:588
  285.1 7.9 %copy-start.26 = (bf16[384,512]{1,0:T(8,128)(2,1)S(1)}, bf16[384,512]{1,0:T(8,128)(2,1)}, u32[]{:S(2)}) copy-start(bf16[384,512]{1,0:T(8,128)(2,1)} %get-tuple-element.82) | copy-start | bytes 1179652
  285.1 9.5 %copy-start.25 = (bf16[384,512]{1,0:T(8,128)(2,1)S(1)}, bf16[384,512]{1,0:T(8,128)(2,1)}, u32[]{:S(2)}) copy-start(bf16[384,512]{1,0:T(8,128)(2,1)} %get-tuple-element.83) | copy-start | bytes 1179652
  285.1 10.8 %copy-start.24 = (bf16[384,512]{1,0:T(8,128)(2,1)S(1)}, bf16[384,512]{1,0:T(8,128)(2,1)}, u32[]{:S(2)}) copy-start(bf16[384,512]{1,0:T(8,128)(2,1)} %get-tuple-element.84) | copy-start | bytes 1179652
  285.1 34.0 %copy-start.15 = (bf16[384,512]{1,0:T(8,128)(2,1)S(1)}, bf16[384,512]{1,0:T(8,128)(2,1)}, u32[]{:S(2)}) copy-start(bf16[384,512]{1,0:T(8,128)(2,1)} %get-tuple-element.81.refs_1_) | copy-start | bytes 1179652
  286.0 35.1 %all-to-all-start.4 = ((f32[64,16,128]{2,1,0:T(8,128)}), f32[64,16,128]{2,1,0:T(8,128)S(1)}, u32[]{:S(2)}, u32[]{:S(2)}) async-start(f32[64,16,128]{2,1,0:T(8,128)} %broadcast_in_dim.8), calls=%async_computation.6 | async-start | bytes 1048576 | tf_op jit(solution)/shard_map/all_to_all | solution.py:584
  292.9 16.5 %collective-permute-start.9 = (bf16[384,512]{1,0:T(8,128)(2,1)S(1)}, bf16[384,512]{1,0:T(8,128)(2,1)S(1)}, u32[]{:S(2)}, u32[]{:S(2)}) collective-permute-start(bf16[384,512]{1,0:T(8,128)(2,1)S(1)} %copy-done.26), channel_id=1, source_target_pairs={{0,3},{1,0},{2,1},{3,2},{4,7},{5,4},{6,5},{7,6},{8,11},{9,8},{10,9... | collective-permute-start | bytes 1179656 | tf_op jit(solution)/shard_map/ppermute | solution.py:588
  294.6 15.8 %collective-permute-start.10 = (bf16[384,512]{1,0:T(8,128)(2,1)S(1)}, bf16[384,512]{1,0:T(8,128)(2,1)S(1)}, u32[]{:S(2)}, u32[]{:S(2)}) collective-permute-start(bf16[384,512]{1,0:T(8,128)(2,1)S(1)} %copy-done.25), channel_id=1, source_target_pairs={{0,2},{1,3},{2,0},{3,1},{4,6},{5,7},{6,4},{7,5},{8,10},{9,11},{10,... | collective-permute-start | bytes 1179656 | tf_op jit(solution)/shard_map/ppermute | solution.py:588
  295.9 23.2 %collective-permute-start.11 = (bf16[384,512]{1,0:T(8,128)(2,1)S(1)}, bf16[384,512]{1,0:T(8,128)(2,1)S(1)}, u32[]{:S(2)}, u32[]{:S(2)}) collective-permute-start(bf16[384,512]{1,0:T(8,128)(2,1)S(1)} %copy-done.24), channel_id=1, source_target_pairs={{0,1},{1,2},{2,3},{3,0},{4,5},{5,6},{6,7},{7,4},{8,9},{9,10},{10,1... | collective-permute-start | bytes 1179656 | tf_op jit(solution)/shard_map/ppermute | solution.py:588
  (5 other events, 5.5 us)
Sparse Core Ops, SparseCore 0:
  9.8 76.8 all-gather.2
  88.5 51.0 all-gather.4
  200.0 45.2 reduce-scatter.2
  248.4 65.7 reduce-scatter.4
where the time goes:
time: 329 us
  waiting for transfers between devices  133 us (40%)
  Pallas kernels  68.9 us (21%)
  starting transfers between devices  60.8 us (18%)
  blocking collectives  46.1 us (14%)
  between operations  14.2 us (4%)
  local copies, waits for them, and re-layouts  4.93 us (1%)
    ppermute x15, waiting for transfers between devices, shift(): lax.ppermute(x, axis, [(i, (i + step) % count) for i in range(count)])  78.6 us
    all_to_all x4, waiting for transfers between devices, swap(): return lax.all_to_all(x, 'expert', split_axis=0, concat_axis=0, tiled=True)  50.3 us
    all_to_all x1, blocking collectives, swap(): return lax.all_to_all(x, 'expert', split_axis=0, concat_axis=0, tiled=True)  46.1 us
    all_to_all x4, starting transfers between devices, swap(): return lax.all_to_all(x, 'expert', split_axis=0, concat_axis=0, tiled=True)  42.4 us
    pallas_call x7, Pallas kernels, staged(): pl.pallas_call(kernel, in_specs=[SCALAR] * len(scalars) + [IN_HBM] * (len...  24.7 us
    ppermute x15, starting transfers between devices, shift(): lax.ppermute(x, axis, [(i, (i + step) % count) for i in range(count)])  18.2 us
    pallas_call x1, Pallas kernels, experts_backward(): pl.pallas_call(backward_body, grid=(CTX,), in_specs=[whole(SLOTS, D), who...  17.4 us
    pallas_call x1, Pallas kernels, experts_forward(): pl.pallas_call(forward_body, grid=(CTX,), in_specs=[whole(EXPERTS, PLAIN,...  15.4 us
  transfers between devices with their start and end apart: 23, of which 14 were waited for; matrix products, arithmetic and copies ran while one was open for 0% of the time, Pallas kernels for 16%

commit v1 on v0

--- a/solution.py
+++ b/solution.py
@@ -339,17 +339,62 @@
     return square, turn
 
 
-def forward_body(
-    arrived, arrived_grads, w_in, w_out, router, own,
-    rows, row_grads, pre_out, y_send,
-    stage, y_sum, branch_grad,
+def forward_body(arrived, w_in, w_out, after, rows, pre_out, y_send, stage, y_sum):
+    step = pl.program_id(0)
+
+    @pl.when(step == 0)
+    def _():
+        from_blocks(arrived, stage, rows, PLAIN)
+        y_sum[...] = jnp.zeros_like(y_sum)
+
+    pre = dot(rows[...], w_in[0])
+    pre_out[0] = pre
+    _, turn = gelu_terms(pre)
+    act = (0.5 * pre * (1.0 + turn)).astype(BF)
+    y_sum[...] += dot(act, w_out[0]).astype(BF).astype(F32)
+
+    @pl.when(step == CTX - 1)
+    def _():
+        ref_to_blocks(y_sum, stage)
+        store_blocks(stage, y_send)
+
+
+def whole(*dims):
+    return pl.BlockSpec(dims, lambda b: (0,) * len(dims))
+
+
+def of_block(*dims):
+    return pl.BlockSpec((1,) + dims, lambda b: (b,) + (0,) * len(dims))
+
+
+def experts_forward(arrived, w_in, w_out, after):
+    return pl.pallas_call(
+        forward_body,
+        grid=(CTX,),
+        in_specs=[whole(EXPERTS, PLAIN, 128), of_block(D, FF_BLOCK), of_block(FF_BLOCK, D), IN_HBM],
+        out_specs=[whole(SLOTS, D), of_block(SLOTS, FF_BLOCK), whole(EXPERTS, PLAIN, 128)],
+        out_shape=[
+            hbm((SLOTS, D), BF),
+            hbm((CTX, SLOTS, FF_BLOCK), F32),
+            hbm((EXPERTS, PLAIN, 128), BF),
+        ],
+        scratch_shapes=[pltpu.VMEM((EXPERTS * PLAIN, 128), F32), pltpu.VMEM((SLOTS, D), F32)],
+        compiler_params=params(60),
+        cost_estimate=cost(10),
+        name="expert_forward",
+    )(arrived, w_in, w_out, after)
+
+
+def backward_body(
+    rows, arrived_grads, pre_in, w_in, w_out, router, own,
+    in_send, out_send, part_send,
+    stage, part_sum, branch_grad, row_grads,
 ):
     step = pl.program_id(0)
 
     @pl.when(step == 0)
     def _():
         from_blocks(arrived_grads.at[:, 0:PLAIN, :], stage, branch_grad, PLAIN)
-        from_blocks(arrived, stage, rows, PLAIN)
         partner_table = arrived_grads[:, PLAIN : PLAIN + 16, :].astype(F32)[:, 0, :]
         partner = jnp.concatenate(
             [partner_table[:, s : s + 1] for s in range(CAP)], axis=0
@@ -357,68 +402,6 @@
         logits = dot_cols(rows[...], router[...])
         margin = jnp.sum(logits * (own[...] - one_hot(partner, EXPERTS)), axis=1, keepdims=True)
         row_grads[...] = (jax.nn.sigmoid(margin) * branch_grad[...].astype(F32)).astype(BF)
-        y_sum[...] = jnp.zeros_like(y_sum)
-
-    pre = dot(rows[...], w_in[0])
-    pre_out[0] = pre
-    _, turn = gelu_terms(pre)
-    act = (0.5 * pre * (1.0 + turn)).astype(BF)
-    y_sum[...] += dot(act, w_out[0]).astype(BF).astype(F32)
-
-    @pl.when(step == CTX - 1)
-    def _():
-        ref_to_blocks(y_sum, stage)
-        store_blocks(stage, y_send)
-
-
-def whole(*dims):
-    return pl.BlockSpec(dims, lambda b: (0,) * len(dims))
-
-
-def of_block(*dims):
-    return pl.BlockSpec((1,) + dims, lambda b: (b,) + (0,) * len(dims))
-
-
-def experts_forward(arrived, arrived_grads, w_in, w_out, router, own):
-    return pl.pallas_call(
-        forward_body,
-        grid=(CTX,),
-        in_specs=[
-            whole(EXPERTS, PLAIN, 128),
-            whole(EXPERTS, TAGGED, 128),
-            of_block(D, FF_BLOCK),
-            of_block(FF_BLOCK, D),
-            whole(EXPERTS, D),
-            whole(1, EXPERTS),
-        ],
-        out_specs=[
-            whole(SLOTS, D),
-            whole(SLOTS, D),
-            of_block(SLOTS, FF_BLOCK),
-            whole(EXPERTS, PLAIN, 128),
-        ],
-        out_shape=[
-            hbm((SLOTS, D), BF),
-            hbm((SLOTS, D), BF),
-            hbm((CTX, SLOTS, FF_BLOCK), F32),
-            hbm((EXPERTS, PLAIN, 128), BF),
-        ],
-        scratch_shapes=[
-            pltpu.VMEM((EXPERTS * PLAIN, 128), F32),
-            pltpu.VMEM((SLOTS, D), F32),
-            pltpu.VMEM((SLOTS, D), BF),
-        ],
-        compiler_params=params(60),
-        cost_estimate=cost(10),
-        name="expert_forward",
-    )(arrived, arrived_grads, w_in, w_out, router, own)
-
-
-def backward_body(rows, row_grads, pre_in, w_in, w_out, in_send, out_send, part_send, stage, part_sum):
-    step = pl.program_id(0)
-
-    @pl.when(step == 0)
-    def _():
         part_sum[...] = jnp.zeros_like(part_sum)
 
     pre = pre_in[0]
@@ -439,16 +422,18 @@
         part_send[:, PLAIN:, :] = jnp.zeros((EXPERTS, CHUNKS, 128), BF)
 
 
-def experts_backward(rows, row_grads, pre, w_in, w_out):
+def experts_backward(rows, arrived_grads, pre, w_in, w_out, router, own):
     return pl.pallas_call(
         backward_body,
         grid=(CTX,),
         in_specs=[
             whole(SLOTS, D),
-            whole(SLOTS, D),
+            whole(EXPERTS, TAGGED, 128),
             of_block(SLOTS, FF_BLOCK),
             of_block(D, FF_BLOCK),
             of_block(FF_BLOCK, D),
+            whole(EXPERTS, D),
+            whole(1, EXPERTS),
         ],
         out_specs=[of_block(D, FF_BLOCK), of_block(FF_BLOCK, D), whole(EXPERTS, TAGGED, 128)],
         out_shape=[
@@ -456,11 +441,16 @@
             hbm((CTX, FF_BLOCK, D), BF),
             hbm((EXPERTS, TAGGED, 128), BF),
         ],
-        scratch_shapes=[pltpu.VMEM((EXPERTS * PLAIN, 128), F32), pltpu.VMEM((SLOTS, D), F32)],
+        scratch_shapes=[
+            pltpu.VMEM((EXPERTS * PLAIN, 128), F32),
+            pltpu.VMEM((SLOTS, D), F32),
+            pltpu.VMEM((SLOTS, D), BF),
+            pltpu.VMEM((SLOTS, D), BF),
+        ],
         compiler_params=params(60),
         cost_estimate=cost(15),
         name="expert_backward",
-    )(rows, row_grads, pre, w_in, w_out)
+    )(rows, arrived_grads, pre, w_in, w_out, router, own)
 
 
 def one_hots(ids):
@@ -611,11 +601,11 @@
         group, attn, resid, mod_scale, mod_shift, router_rows, expert_ids, place
     )
     arrived = swap(rows)
-    flat_rows, flat_grads, pre_act, y_rows = experts_forward(
-        arrived, arrived_grads, full_in, full_out, router_rows, own
-    )
+    flat_rows, pre_act, y_rows = experts_forward(arrived, full_in, full_out, arrived_grads)
     outputs = swap(y_rows)
-    in_terms, out_terms, part_rows = experts_backward(flat_rows, flat_grads, pre_act, full_in, full_out)
+    in_terms, out_terms, part_rows = experts_backward(
+        flat_rows, arrived_grads, pre_act, full_in, full_out, router_rows, own
+    )
     in_terms, out_terms, _ = lax.optimization_barrier((in_terms, out_terms, outputs))
     grad_w_in, grad_w_out = (
         lax.psum_scatter(x, "ctx", scatter_dimension=0, tiled=True) for x in (in_terms, out_terms)

time: 329 us -> 327 us (level)
  blocking collectives: 46.1 us -> 91.6 us
  waiting for transfers between devices: 133 us -> 97.2 us
  starting transfers between devices: 60.8 us -> 49.6 us
    all_to_all x1 -> x2, blocking collectives: 46.1 us -> 91.6 us  [swap(): return lax.all_to_all(x, 'expert', split_axis=0, concat_axis=0, tiled=True)]
    all_to_all x4 -> x3, waiting for transfers between devices: 50.3 us -> 14.3 us  [swap(): return lax.all_to_all(x, 'expert', split_axis=0, concat_axis=0, tiled=True)]
    all_to_all x4 -> x3, starting transfers between devices: 42.4 us -> 31.3 us  [swap(): return lax.all_to_all(x, 'expert', split_axis=0, concat_axis=0, tiled=True)]
  transfers between devices with their start and end apart: 23 -> 22, of which waited for: 14 -> 13; matrix products, arithmetic and copies ran while one was open for 0% -> 0% of each run, Pallas kernels for 16% -> 17%
where the time goes in v1:
time: 327 us; the launch traced here: 326 us
  waiting for transfers between devices  97.2 us (30%)
  blocking collectives  91.6 us (28%)
  Pallas kernels  68.1 us (21%)
  starting transfers between devices  49.6 us (15%)
  between operations  14.2 us (4%)
  local copies, waits for them, and re-layouts  4.94 us (2%)
    all_to_all x2, blocking collectives, swap(): return lax.all_to_all(x, 'expert', split_axis=0, concat_axis=0, tiled=True)  91.6 us
    ppermute x15, waiting for transfers between devices, shift(): lax.ppermute(x, axis, [(i, (i + step) % count) for i in range(count)])  78.6 us
    all_to_all x3, starting transfers between devices, swap(): return lax.all_to_all(x, 'expert', split_axis=0, concat_axis=0, tiled=True)  31.3 us
    pallas_call x7, Pallas kernels, staged(): pl.pallas_call(kernel, in_specs=[SCALAR] * len(scalars) + [IN_HBM] * (len...  24.8 us
    pallas_call x1, Pallas kernels, experts_backward(): pl.pallas_call(backward_body, grid=(CTX,), in_specs=[whole(SLOTS, D), who...  19.3 us
    ppermute x15, starting transfers between devices, shift(): lax.ppermute(x, axis, [(i, (i + step) % count) for i in range(count)])  18.2 us
    all_to_all x3, waiting for transfers between devices, swap(): return lax.all_to_all(x, 'expert', split_axis=0, concat_axis=0, tiled=True)  14.3 us
    pallas_call x1, Pallas kernels, experts_forward(): pl.pallas_call(forward_body, grid=(CTX,), in_specs=[whole(EXPERTS, PLAIN,...  12.7 us
  transfers between devices with their start and end apart: 22, of which 13 were waited for; matrix products, arithmetic and copies ran while one was open for 0% of the time, Pallas kernels for 17%

profile of v1, /device:TPU:1, one launch (start us, length us, event | category | flops | bytes accessed | tf_op | source)
XLA Modules:
  0.0 326.2 jit_solution(1264679675704201538)
XLA Ops:
  7.3 0.7 all-gather.3.cloned.1.call-update
  8.0 0.7 all-gather.5.cloned.1.call-update
  8.9 1.4 pack_heads.1
  10.4 1.0 copy-done.4
  11.4 4.1 %dispatch_grads.1 = (s32[128,2]{1,0:T(8,128)}, bf16[64,96,128]{2,1,0:T(8,128)(2,1)}) custom-call(bf16[128,2048]{1,0:T(8,128)(2,1)S(1)} %copy-done.1, f32[1,2048]{1,0:T(1,128)S(1)} %copy-done.17, s32[128,2]{1,0:T(8,128)S(1)} %copy.25.refs_2_.refs_9_, bf16[384,512]{1,0:T(8,128)(2,1)S(1)} %copy-done.4), custom_call_target="tpu_custom_call" | custom-call | bytes 9000000 | tf_op jit(solution)/shard_map/dispatch_grads/pallas_call | solution.py:90
  15.5 13.5 %all-to-all-start.1 = ((bf16[64,96,128]{2,1,0:T(8,128)(2,1)}), bf16[64,96,128]{2,1,0:T(8,128)(2,1)}, u32[]{:S(2)}, u32[]{:S(2)}) async-start(bf16[64,96,128]{2,1,0:T(8,128)(2,1)} %get-tuple-element.62), calls=%async_computation.1 | async-start | bytes 3145728 | tf_op jit(solution)/shard_map/all_to_all | solution.py:574
  29.0 1.3 collective-permute-start
  30.3 2.4 collective-permute-start.1
  32.8 1.2 collective-permute-start.2
  33.9 15.7 %collective-permute-done.refs_1_ = bf16[384,512]{1,0:T(8,128)(2,1)S(1)} collective-permute-done((bf16[384,512]{1,0:T(8,128)(2,1)S(1)}, bf16[384,512]{1,0:T(8,128)(2,1)S(1)}, u32[]{:S(2)}, u32[]{:S(2)}) %collective-permute-start) | collective-permute-done | bytes 393248 | tf_op jit(solution)/shard_map/ppermute | solution.py:578
  49.6 17.8 %collective-permute-done.1.refs_2_ = bf16[384,512]{1,0:T(8,128)(2,1)S(1)} collective-permute-done((bf16[384,512]{1,0:T(8,128)(2,1)S(1)}, bf16[384,512]{1,0:T(8,128)(2,1)S(1)}, u32[]{:S(2)}, u32[]{:S(2)}) %collective-permute-start.1) | collective-permute-done | bytes 393248 | tf_op jit(solution)/shard_map/ppermute | solution.py:578
  67.5 4.6 %attend_forward.1 = (bf16[128,512]{1,0:T(8,128)(2,1)}, bf16[128,512]{1,0:T(8,128)(2,1)}, bf16[128,512]{1,0:T(8,128)(2,1)}, bf16[128,512]{1,0:T(8,128)(2,1)}, bf16[4,512,512]{2,1,0:T(8,128)(2,1)}) custom-call(bf16[384,512]{1,0:T(8,128)(2,1)S(1)} %copy-done.5, bf16[384,512]{1,0:T(8,128)(2,1)S(1)} %collective-permute-done.refs_1_, ...), custom_call_target="tpu_custom_call" | custom-call | bytes 30000000 | tf_op jit(solution)/shard_map/attend_forward/pallas_call | solution.py:246
  72.3 2.0 collective-permute-start.4
  74.3 0.9 collective-permute-start.5
  75.1 5.0 %collective-permute-done.3.refs_2_.refs_3_ = bf16[128,512]{1,0:T(8,128)(2,1)S(1)} collective-permute-done((bf16[128,512]{1,0:T(8,128)(2,1)}, bf16[128,512]{1,0:T(8,128)(2,1)S(1)}, u32[]{:S(2)}, u32[]{:S(2)}) %collective-permute-start.3) | collective-permute-done | bytes 131104 | tf_op jit(solution)/shard_map/ppermute | solution.py:578
  80.1 1.4 collective-permute-done.4.refs_3_.refs_4_
  81.5 4.4 %collective-permute-done.5.refs_4_.refs_5_ = bf16[128,512]{1,0:T(8,128)(2,1)S(1)} collective-permute-done((bf16[128,512]{1,0:T(8,128)(2,1)}, bf16[128,512]{1,0:T(8,128)(2,1)S(1)}, u32[]{:S(2)}, u32[]{:S(2)}) %collective-permute-start.5) | collective-permute-done | bytes 131104 | tf_op jit(solution)/shard_map/ppermute | solution.py:578
  86.0 0.9 copy-done.6
  86.9 4.7 %norm_dispatch.1 = (bf16[64,80,128]{2,1,0:T(8,128)(2,1)}, bf16[128,2048]{1,0:T(8,128)(2,1)}, f32[128,128]{1,0:T(8,128)}, f32[128,128]{1,0:T(8,128)}) custom-call(s32[1]{0:T(128)} %bitcast.refs_0_, bf16[128,512]{1,0:T(8,128)(2,1)S(1)} %copy-done.6, bf16[128,512]{1,0:T(8,128)(2,1)S(1)} %collective-permute-done.3.refs_2_.refs_3_, ...), custom_call_target="tpu_custom_call" | custom-call | bytes 9000000 | tf_op jit(solution)/shard_map/norm_dispatch/pallas_call | solution.py:90
  91.6 45.6 %all_to_all.25.arrived = bf16[64,80,128]{2,1,0:T(8,128)(2,1)} all-to-all(bf16[64,80,128]{2,1,0:T(8,128)(2,1)} %get-tuple-element.61), channel_id=1, replica_groups=mesh['expert'=64,'ctx'=4] {'expert'}, dimensions={0} | all-to-all | bytes 2621440 | tf_op jit(solution)/shard_map/all_to_all | solution.py:574
  137.2 2.4 all-gather.5.cloned.1.call-done.w_out
  139.6 12.7 %expert_forward.1 = (bf16[320,2048]{1,0:T(8,128)(2,1)}, f32[4,320,256]{2,1,0:T(8,128)}, bf16[64,80,128]{2,1,0:T(8,128)(2,1)}) custom-call(bf16[64,80,128]{2,1,0:T(8,128)(2,1)} %all_to_all.25.arrived, bf16[4,2048,256]{2,1,0:T(8,128)(2,1)} %all-gather.3.cloned.1.call-done.w_in, bf16[4,256,2048]{2,1,0:T(8,128)(2,1)} %all-gather.5.cloned.1.call-done.w_out, ...), custom_call_target="tpu_custom_call" | custom-call | bytes 30000000 | tf_op jit(solution)/shard_map/expert_forward/pallas_call | solution.py:371
  152.3 10.9 %all-to-all-start.2 = ((bf16[64,80,128]{2,1,0:T(8,128)(2,1)}), bf16[64,80,128]{2,1,0:T(8,128)(2,1)S(1)}, u32[]{:S(2)}, u32[]{:S(2)}) async-start(bf16[64,80,128]{2,1,0:T(8,128)(2,1)} %get-tuple-element.63), calls=%async_computation.2 | async-start | bytes 2621440 | tf_op jit(solution)/shard_map/all_to_all | solution.py:574
  163.7 19.3 %expert_backward.1 = (bf16[4,2048,256]{2,1,0:T(8,128)(2,1)}, bf16[4,256,2048]{2,1,0:T(8,128)(2,1)}, bf16[64,96,128]{2,1,0:T(8,128)(2,1)}) custom-call(bf16[320,2048]{1,0:T(8,128)(2,1)} %get-tuple-element.66.rows, bf16[64,96,128]{2,1,0:T(8,128)(2,1)} %all-to-all-done.1.after.arrived_grads, f32[4,320,256]{2,1,0:T(8,128)} %get-tuple-element.67.pre_in, ...), custom_call_target="tpu_custom_call" | custom-call | bytes 45000000 | tf_op jit(solution)/shard_map/expert_backward/pallas_call | solution.py:426
  183.1 14.3 %all-to-all-done.2.refs_1_ = bf16[64,80,128]{2,1,0:T(8,128)(2,1)S(1)} async-done(((bf16[64,80,128]{2,1,0:T(8,128)(2,1)}), bf16[64,80,128]{2,1,0:T(8,128)(2,1)S(1)}, u32[]{:S(2)}, u32[]{:S(2)}) %all-to-all-start.2) | async-done | bytes 1310752 | tf_op jit(solution)/shard_map/all_to_all | solution.py:574
  197.4 1.1 copy-done.20
  199.0 6.4 %mixed_output.1 = (bf16[128,2048]{1,0:T(8,128)(2,1)}, bf16[128,64]{1,0:T(8,128)(2,1)}, bf16[64,96,128]{2,1,0:T(8,128)(2,1)}) custom-call(s32[1]{0:T(128)} %bitcast.refs_0_, bf16[64,80,128]{2,1,0:T(8,128)(2,1)} %copy-done.20, bf16[128,512]{1,0:T(8,128)(2,1)} %get-tuple-element.56.refs_1_.refs_2_, ...), custom_call_target="tpu_custom_call", output_to_operand_aliasing={{2}: (13, {})} | custom-call | bytes 15000000 | tf_op jit(solution)/shard_map/mixed_output/pallas_call | solution.py:90
  205.4 46.1 %all_to_all.26.refs_1_ = bf16[64,96,128]{2,1,0:T(8,128)(2,1)} all-to-all(bf16[64,96,128]{2,1,0:T(8,128)(2,1)} %get-tuple-element.70), channel_id=1, replica_groups=mesh['expert'=64,'ctx'=4] {'expert'}, dimensions={0} | all-to-all | bytes 3145728 | tf_op jit(solution)/shard_map/all_to_all | solution.py:574
  251.4 5.1 %resid_backward.1 = (bf16[128,2048]{1,0:T(8,128)(2,1)}, f32[16,128]{1,0:T(8,128)}, bf16[128,512]{1,0:T(8,128)(2,1)}, bf16[128,512]{1,0:T(8,128)(2,1)}, bf16[128,...) custom-call(s32[1]{0:T(128)} %bitcast.refs_0_, bf16[64,96,128]{2,1,0:T(8,128)(2,1)} %all_to_all.26.refs_1_, ...), custom_call_target="tpu_custom_call" | custom-call | bytes 90000000 | tf_op jit(solution)/shard_map/resid_backward/pallas_call | solution.py:90
  257.2 1.5 collective-permute-start.7
  258.7 1.8 collective-permute-start.8
  260.5 5.7 %collective-permute-done.6.refs_1_ = bf16[128,512]{1,0:T(8,128)(2,1)S(1)} collective-permute-done((bf16[128,512]{1,0:T(8,128)(2,1)}, bf16[128,512]{1,0:T(8,128)(2,1)S(1)}, u32[]{:S(2)}, u32[]{:S(2)}) %collective-permute-start.6) | collective-permute-done | bytes 131104 | tf_op jit(solution)/shard_map/ppermute | solution.py:578
  266.2 4.2 %collective-permute-done.7.refs_2_ = bf16[128,512]{1,0:T(8,128)(2,1)S(1)} collective-permute-done((bf16[128,512]{1,0:T(8,128)(2,1)}, bf16[128,512]{1,0:T(8,128)(2,1)S(1)}, u32[]{:S(2)}, u32[]{:S(2)}) %collective-permute-start.7) | collective-permute-done | bytes 131104 | tf_op jit(solution)/shard_map/ppermute | solution.py:578
  270.5 1.9 collective-permute-done.8.refs_3_
  272.6 1.4 collective-permute-start.13
  274.1 0.9 collective-permute-start.12
  274.9 0.9 copy-done.16
  275.8 6.7 %attend_backward.1 = (bf16[384,512]{1,0:T(8,128)(2,1)}, bf16[384,512]{1,0:T(8,128)(2,1)}, bf16[384,512]{1,0:T(8,128)(2,1)}, bf16[384,512]{1,0:T(8,128)(2,1)}) custom-call(bf16[4,512,512]{2,1,0:T(8,128)(2,1)S(1)} %copy-done.3, bf16[128,512]{1,0:T(8,128)(2,1)S(1)} %copy-done.16, bf16[128,512]{1,0:T(8,128)(2,1)S(1)} %collective-permute-done.6.refs_1_, ...), custom_call_target="tpu_custom_call" | custom-call | bytes 300000000 | tf_op jit(solution)/shard_map/attend_backward/pallas_call | solution.py:279
  282.6 0.8 broadcast_in_dim.8
  283.5 6.9 %all-to-all-start.4 = ((f32[64,16,128]{2,1,0:T(8,128)}), f32[64,16,128]{2,1,0:T(8,128)S(1)}, u32[]{:S(2)}, u32[]{:S(2)}) async-start(f32[64,16,128]{2,1,0:T(8,128)} %broadcast_in_dim.8), calls=%async_computation.6 | async-start | bytes 1048576 | tf_op jit(solution)/shard_map/all_to_all | solution.py:574
  290.4 1.7 collective-permute-start.9
  292.1 1.3 collective-permute-start.10
  293.4 0.8 collective-permute-start.11
  294.2 12.8 %collective-permute-done.9.refs_2_ = bf16[384,512]{1,0:T(8,128)(2,1)S(1)} collective-permute-done((bf16[384,512]{1,0:T(8,128)(2,1)S(1)}, bf16[384,512]{1,0:T(8,128)(2,1)S(1)}, u32[]{:S(2)}, u32[]{:S(2)}) %collective-permute-start.9) | collective-permute-done | bytes 393248 | tf_op jit(solution)/shard_map/ppermute | solution.py:578
  306.9 1.0 collective-permute-done.10.refs_3_
  307.9 8.6 %collective-permute-done.11.refs_4_ = bf16[384,512]{1,0:T(8,128)(2,1)S(1)} collective-permute-done((bf16[384,512]{1,0:T(8,128)(2,1)S(1)}, bf16[384,512]{1,0:T(8,128)(2,1)S(1)}, u32[]{:S(2)}, u32[]{:S(2)}) %collective-permute-start.11) | collective-permute-done | bytes 393248 | tf_op jit(solution)/shard_map/ppermute | solution.py:578
  316.6 2.0 unpack_heads.1
  318.6 1.0 order_router.1
  (75 shorter events, 2.7 us)
Async XLA Ops:
  7.2 1.6 copy-start.22
  7.2 1.7 copy-start.14
  7.2 1.7 copy-start.13
  7.2 1.7 copy-start.12
  7.2 130.0 %all-gather.3.cloned.1.call-start = ((), (), s32[]{:S(2)}) async-start(), calls=%async_computation.7 | async-start | bytes 5242880 | tf_op jit(solution)/shard_map/all_gather | solution.py:596
  7.9 2.4 copy-start.1
  8.0 2.4 copy-start.17
  8.0 131.6 %all-gather.5.cloned.1.call-start = ((), (), s32[]{:S(2)}) async-start(), calls=%async_computation.8 | async-start | bytes 5242880 | tf_op jit(solution)/shard_map/all_gather | solution.py:597
  8.8 77.1 %copy-start.10 = (s32[128,2]{1,0:T(8,128)}, s32[128,2]{1,0:T(8,128)S(1)}, u32[]{:S(2)}) copy-start(s32[128,2]{1,0:T(8,128)S(1)} %copy.25.refs_2_.refs_9_) | copy-start | bytes 3076
  15.4 13.6 %copy-start.28 = (bf16[384,512]{1,0:T(8,128)(2,1)S(1)}, bf16[384,512]{1,0:T(8,128)(2,1)}, u32[]{:S(2)}) copy-start(bf16[384,512]{1,0:T(8,128)(2,1)} %get-tuple-element.53) | copy-start | bytes 1179652
  15.4 14.9 %copy-start.27 = (bf16[384,512]{1,0:T(8,128)(2,1)S(1)}, bf16[384,512]{1,0:T(8,128)(2,1)}, u32[]{:S(2)}) copy-start(bf16[384,512]{1,0:T(8,128)(2,1)} %get-tuple-element.54) | copy-start | bytes 1179652
  15.4 17.3 %copy-start.26 = (bf16[384,512]{1,0:T(8,128)(2,1)S(1)}, bf16[384,512]{1,0:T(8,128)(2,1)}, u32[]{:S(2)}) copy-start(bf16[384,512]{1,0:T(8,128)(2,1)} %get-tuple-element.55) | copy-start | bytes 1179652
  15.5 52.0 %copy-start.5 = (bf16[384,512]{1,0:T(8,128)(2,1)S(1)}, bf16[384,512]{1,0:T(8,128)(2,1)}, u32[]{:S(2)}) copy-start(bf16[384,512]{1,0:T(8,128)(2,1)} %get-tuple-element.52.refs_0_.refs_3_) | copy-start | bytes 1179652
  15.5 76.1 %all-to-all-start.1 = ((bf16[64,96,128]{2,1,0:T(8,128)(2,1)}), bf16[64,96,128]{2,1,0:T(8,128)(2,1)}, u32[]{:S(2)}, u32[]{:S(2)}) async-start(bf16[64,96,128]{2,1,0:T(8,128)(2,1)} %get-tuple-element.62), calls=%async_computation.1 | async-start | bytes 3145728 | tf_op jit(solution)/shard_map/all_to_all | solution.py:574
  28.9 57.0 %copy-start = (bf16[128,2048]{1,0:T(8,128)(2,1)S(1)}, bf16[128,2048]{1,0:T(8,128)(2,1)}, u32[]{:S(2)}) copy-start(bf16[128,2048]{1,0:T(8,128)(2,1)} %refs_6_.5) | copy-start | bytes 1572868
  29.0 57.0 %copy-start.2 = (bf16[2048,64]{0,1:T(8,128)(2,1)S(1)}, bf16[2048,64]{0,1:T(8,128)(2,1)}, u32[]{:S(2)}) copy-start(bf16[2048,64]{0,1:T(8,128)(2,1)} %param.19) | copy-start | bytes 786436
  29.0 57.0 %copy-start.11 = (s32[128,2]{1,0:T(8,128)S(1)}, s32[128,2]{1,0:T(8,128)}, u32[]{:S(2)}) copy-start(s32[128,2]{1,0:T(8,128)} %get-tuple-element.60.refs_10_) | copy-start | bytes 3076
  29.0 57.0 %copy-start.18 = (f32[1,2048]{1,0:T(1,128)S(1)}, f32[1,2048]{1,0:T(1,128)}, u32[]{:S(2)}) copy-start(f32[1,2048]{1,0:T(1,128)} %refs_8_.3) | copy-start | bytes 24580
  29.0 57.0 %copy-start.19 = (f32[1,2048]{1,0:T(1,128)S(1)}, f32[1,2048]{1,0:T(1,128)}, u32[]{:S(2)}) copy-start(f32[1,2048]{1,0:T(1,128)} %refs_7_.3) | copy-start | bytes 24580
  29.0 20.6 %collective-permute-start = (bf16[384,512]{1,0:T(8,128)(2,1)S(1)}, bf16[384,512]{1,0:T(8,128)(2,1)S(1)}, u32[]{:S(2)}, u32[]{:S(2)}) collective-permute-start(bf16[384,512]{1,0:T(8,128)(2,1)S(1)} %copy-done.28), channel_id=1, source_target_pairs={{0,1},{1,2},{2,3},{3,0},{4,5},{5,6},{6,7},{7,4},{8,9},{9,10},{10,1... | collective-permute-start | bytes 1179656 | tf_op jit(solution)/shard_map/ppermute | solution.py:578
  30.3 37.1 %collective-permute-start.1 = (bf16[384,512]{1,0:T(8,128)(2,1)S(1)}, bf16[384,512]{1,0:T(8,128)(2,1)S(1)}, u32[]{:S(2)}, u32[]{:S(2)}) collective-permute-start(bf16[384,512]{1,0:T(8,128)(2,1)S(1)} %copy-done.27), channel_id=1, source_target_pairs={{0,2},{1,3},{2,0},{3,1},{4,6},{5,7},{6,4},{7,5},{8,10},{9,11},{10,... | collective-permute-start | bytes 1179656 | tf_op jit(solution)/shard_map/ppermute | solution.py:578
  32.8 34.7 %collective-permute-start.2 = (bf16[384,512]{1,0:T(8,128)(2,1)S(1)}, bf16[384,512]{1,0:T(8,128)(2,1)S(1)}, u32[]{:S(2)}, u32[]{:S(2)}) collective-permute-start(bf16[384,512]{1,0:T(8,128)(2,1)S(1)} %copy-done.26), channel_id=1, source_target_pairs={{0,3},{1,0},{2,1},{3,2},{4,7},{5,4},{6,5},{7,6},{8,11},{9,8},{10,9... | collective-permute-start | bytes 1179656 | tf_op jit(solution)/shard_map/ppermute | solution.py:578
  72.0 8.0 %collective-permute-start.3 = (bf16[128,512]{1,0:T(8,128)(2,1)}, bf16[128,512]{1,0:T(8,128)(2,1)S(1)}, u32[]{:S(2)}, u32[]{:S(2)}) collective-permute-start(bf16[128,512]{1,0:T(8,128)(2,1)} %get-tuple-element.57), channel_id=1, source_target_pairs={{0,3},{1,0},{2,1},{3,2},{4,7},{5,4},{6,5},{7,6},{8,11},{9,8},{10,9... | collective-permute-start | bytes 393224 | tf_op jit(solution)/shard_map/ppermute | solution.py:578
  72.3 9.2 %collective-permute-start.4 = (bf16[128,512]{1,0:T(8,128)(2,1)}, bf16[128,512]{1,0:T(8,128)(2,1)S(1)}, u32[]{:S(2)}, u32[]{:S(2)}) collective-permute-start(bf16[128,512]{1,0:T(8,128)(2,1)} %get-tuple-element.58), channel_id=1, source_target_pairs={{0,2},{1,3},{2,0},{3,1},{4,6},{5,7},{6,4},{7,5},{8,10},{9,11},{10,... | collective-permute-start | bytes 393224 | tf_op jit(solution)/shard_map/ppermute | solution.py:578
  74.3 11.6 %collective-permute-start.5 = (bf16[128,512]{1,0:T(8,128)(2,1)}, bf16[128,512]{1,0:T(8,128)(2,1)S(1)}, u32[]{:S(2)}, u32[]{:S(2)}) collective-permute-start(bf16[128,512]{1,0:T(8,128)(2,1)} %get-tuple-element.59), channel_id=1, source_target_pairs={{0,1},{1,2},{2,3},{3,0},{4,5},{5,6},{6,7},{7,4},{8,9},{9,10},{10,1... | collective-permute-start | bytes 393224 | tf_op jit(solution)/shard_map/ppermute | solution.py:578
  80.1 57.1 %copy-start.7 = (bf16[128,512]{1,0:T(8,128)(2,1)}, bf16[128,512]{1,0:T(8,128)(2,1)S(1)}, u32[]{:S(2)}) copy-start(bf16[128,512]{1,0:T(8,128)(2,1)S(1)} %collective-permute-done.3.refs_2_.refs_3_) | copy-start | bytes 393220
  81.5 55.7 %copy-start.8 = (bf16[128,512]{1,0:T(8,128)(2,1)}, bf16[128,512]{1,0:T(8,128)(2,1)S(1)}, u32[]{:S(2)}) copy-start(bf16[128,512]{1,0:T(8,128)(2,1)S(1)} %collective-permute-done.4.refs_3_.refs_4_) | copy-start | bytes 393220
  85.9 51.3 %copy-start.9 = (bf16[128,512]{1,0:T(8,128)(2,1)}, bf16[128,512]{1,0:T(8,128)(2,1)S(1)}, u32[]{:S(2)}) copy-start(bf16[128,512]{1,0:T(8,128)(2,1)S(1)} %collective-permute-done.5.refs_4_.refs_5_) | copy-start | bytes 393220
  152.3 45.1 %all-to-all-start.2 = ((bf16[64,80,128]{2,1,0:T(8,128)(2,1)}), bf16[64,80,128]{2,1,0:T(8,128)(2,1)S(1)}, u32[]{:S(2)}, u32[]{:S(2)}) async-start(bf16[64,80,128]{2,1,0:T(8,128)(2,1)} %get-tuple-element.63), calls=%async_computation.2 | async-start | bytes 2621440 | tf_op jit(solution)/shard_map/all_to_all | solution.py:574
  163.2 156.5 %reduce-scatter.3.cloned.1.call-start = ((), (), s32[]{:S(2)}) async-start(), calls=%async_computation.9 | async-start | bytes 5242880 | tf_op jit(solution)/shard_map/reduce_scatter | solution.py:611
  197.3 1.1 copy-start.20
  198.4 121.3 %reduce-scatter.5.cloned.1.call-start = ((), (), s32[]{:S(2)}) async-start(), calls=%async_computation.10 | async-start | bytes 5242880 | tf_op jit(solution)/shard_map/reduce_scatter | solution.py:611
  251.4 23.5 %copy-start.3 = (bf16[4,512,512]{2,1,0:T(8,128)(2,1)S(1)}, bf16[4,512,512]{2,1,0:T(8,128)(2,1)}, u32[]{:S(2)}) copy-start(bf16[4,512,512]{2,1,0:T(8,128)(2,1)} %get-tuple-element.74.saved) | copy-start | bytes 6291460
  256.6 26.1 %copy-start.21 = (f32[16,128]{1,0:T(8,128)S(1)}, f32[16,128]{1,0:T(8,128)}, u32[]{:S(2)}) copy-start(f32[16,128]{1,0:T(8,128)} %get-tuple-element.92) | copy-start | bytes 24580
  256.6 9.7 %collective-permute-start.6 = (bf16[128,512]{1,0:T(8,128)(2,1)}, bf16[128,512]{1,0:T(8,128)(2,1)S(1)}, u32[]{:S(2)}, u32[]{:S(2)}) collective-permute-start(bf16[128,512]{1,0:T(8,128)(2,1)} %get-tuple-element.76), channel_id=1, source_target_pairs={{0,1},{1,2},{2,3},{3,0},{4,5},{5,6},{6,7},{7,4},{8,9},{9,10},{10,1... | collective-permute-start | bytes 393224 | tf_op jit(solution)/shard_map/ppermute | solution.py:578
  257.2 13.3 %collective-permute-start.7 = (bf16[128,512]{1,0:T(8,128)(2,1)}, bf16[128,512]{1,0:T(8,128)(2,1)S(1)}, u32[]{:S(2)}, u32[]{:S(2)}) collective-permute-start(bf16[128,512]{1,0:T(8,128)(2,1)} %get-tuple-element.77), channel_id=1, source_target_pairs={{0,2},{1,3},{2,0},{3,1},{4,6},{5,7},{6,4},{7,5},{8,10},{9,11},{10,... | collective-permute-start | bytes 393224 | tf_op jit(solution)/shard_map/ppermute | solution.py:578
  258.7 13.6 %collective-permute-start.8 = (bf16[128,512]{1,0:T(8,128)(2,1)}, bf16[128,512]{1,0:T(8,128)(2,1)S(1)}, u32[]{:S(2)}, u32[]{:S(2)}) collective-permute-start(bf16[128,512]{1,0:T(8,128)(2,1)} %get-tuple-element.78), channel_id=1, source_target_pairs={{0,3},{1,0},{2,1},{3,2},{4,7},{5,4},{6,5},{7,6},{8,11},{9,8},{10,9... | collective-permute-start | bytes 393224 | tf_op jit(solution)/shard_map/ppermute | solution.py:578
  272.4 10.2 %collective-permute-start.14 = (f32[16,128]{1,0:T(8,128)}, f32[16,128]{1,0:T(8,128)S(1)}, u32[]{:S(2)}, u32[]{:S(2)}) collective-permute-start(f32[16,128]{1,0:T(8,128)} %get-tuple-element.92), channel_id=1, source_target_pairs={{0,3},{1,0},{2,1},{3,2},{4,7},{5,4},{6,5},{7,6},{8,11},{9,8},{10,9... | collective-permute-start | bytes 24584 | tf_op jit(solution)/shard_map/ppermute | solution.py:578
  272.6 10.0 %collective-permute-start.13 = (f32[16,128]{1,0:T(8,128)}, f32[16,128]{1,0:T(8,128)S(1)}, u32[]{:S(2)}, u32[]{:S(2)}) collective-permute-start(f32[16,128]{1,0:T(8,128)} %get-tuple-element.92), channel_id=1, source_target_pairs={{0,2},{1,3},{2,0},{3,1},{4,6},{5,7},{6,4},{7,5},{8,10},{9,11},{10,... | collective-permute-start | bytes 24584 | tf_op jit(solution)/shard_map/ppermute | solution.py:578
  274.1 8.5 %collective-permute-start.12 = (f32[16,128]{1,0:T(8,128)}, f32[16,128]{1,0:T(8,128)S(1)}, u32[]{:S(2)}, u32[]{:S(2)}) collective-permute-start(f32[16,128]{1,0:T(8,128)} %get-tuple-element.92), channel_id=1, source_target_pairs={{0,1},{1,2},{2,3},{3,0},{4,5},{5,6},{6,7},{7,4},{8,9},{9,10},{10,1... | collective-permute-start | bytes 24584 | tf_op jit(solution)/shard_map/ppermute | solution.py:578
  282.6 7.9 %copy-start.25 = (bf16[384,512]{1,0:T(8,128)(2,1)S(1)}, bf16[384,512]{1,0:T(8,128)(2,1)}, u32[]{:S(2)}) copy-start(bf16[384,512]{1,0:T(8,128)(2,1)} %get-tuple-element.80) | copy-start | bytes 1179652
  282.6 9.5 %copy-start.24 = (bf16[384,512]{1,0:T(8,128)(2,1)S(1)}, bf16[384,512]{1,0:T(8,128)(2,1)}, u32[]{:S(2)}) copy-start(bf16[384,512]{1,0:T(8,128)(2,1)} %get-tuple-element.81) | copy-start | bytes 1179652
  282.6 10.8 %copy-start.23 = (bf16[384,512]{1,0:T(8,128)(2,1)S(1)}, bf16[384,512]{1,0:T(8,128)(2,1)}, u32[]{:S(2)}) copy-start(bf16[384,512]{1,0:T(8,128)(2,1)} %get-tuple-element.82) | copy-start | bytes 1179652
  282.6 34.0 %copy-start.15 = (bf16[384,512]{1,0:T(8,128)(2,1)S(1)}, bf16[384,512]{1,0:T(8,128)(2,1)}, u32[]{:S(2)}) copy-start(bf16[384,512]{1,0:T(8,128)(2,1)} %get-tuple-element.79.refs_1_) | copy-start | bytes 1179652
  283.5 35.1 %all-to-all-start.4 = ((f32[64,16,128]{2,1,0:T(8,128)}), f32[64,16,128]{2,1,0:T(8,128)S(1)}, u32[]{:S(2)}, u32[]{:S(2)}) async-start(f32[64,16,128]{2,1,0:T(8,128)} %broadcast_in_dim.8), calls=%async_computation.6 | async-start | bytes 1048576 | tf_op jit(solution)/shard_map/all_to_all | solution.py:574
  290.4 16.5 %collective-permute-start.9 = (bf16[384,512]{1,0:T(8,128)(2,1)S(1)}, bf16[384,512]{1,0:T(8,128)(2,1)S(1)}, u32[]{:S(2)}, u32[]{:S(2)}) collective-permute-start(bf16[384,512]{1,0:T(8,128)(2,1)S(1)} %copy-done.25), channel_id=1, source_target_pairs={{0,3},{1,0},{2,1},{3,2},{4,7},{5,4},{6,5},{7,6},{8,11},{9,8},{10,9... | collective-permute-start | bytes 1179656 | tf_op jit(solution)/shard_map/ppermute | solution.py:578
  292.1 15.8 %collective-permute-start.10 = (bf16[384,512]{1,0:T(8,128)(2,1)S(1)}, bf16[384,512]{1,0:T(8,128)(2,1)S(1)}, u32[]{:S(2)}, u32[]{:S(2)}) collective-permute-start(bf16[384,512]{1,0:T(8,128)(2,1)S(1)} %copy-done.24), channel_id=1, source_target_pairs={{0,2},{1,3},{2,0},{3,1},{4,6},{5,7},{6,4},{7,5},{8,10},{9,11},{10,... | collective-permute-start | bytes 1179656 | tf_op jit(solution)/shard_map/ppermute | solution.py:578
  293.4 23.2 %collective-permute-start.11 = (bf16[384,512]{1,0:T(8,128)(2,1)S(1)}, bf16[384,512]{1,0:T(8,128)(2,1)S(1)}, u32[]{:S(2)}, u32[]{:S(2)}) collective-permute-start(bf16[384,512]{1,0:T(8,128)(2,1)S(1)} %copy-done.23), channel_id=1, source_target_pairs={{0,1},{1,2},{2,3},{3,0},{4,5},{5,6},{6,7},{7,4},{8,9},{9,10},{10,1... | collective-permute-start | bytes 1179656 | tf_op jit(solution)/shard_map/ppermute | solution.py:578
  (3 other events, 2.8 us)
Sparse Core Ops, SparseCore 0:
  9.8 76.7 all-gather.2
  88.5 51.0 all-gather.4
  197.5 45.2 reduce-scatter.2
  245.9 65.7 reduce-scatter.4
